TPU v7x, 32 devices: a whole 2x2x4 slice. The times are simulated.
32 devices in a mesh: group: 2 (over y), tm: 8 (over z, core), pix: 2 (over x), sub: 1.
Axes of the slice: x: 2, y: 2, z: 4, core: 2. Of those that a mesh axis runs over, the one named last changes fastest.
Arguments:
- anomaly: bfloat16 [512, 65536], P('tm', ('group', 'pix', 'sub')), parts along dimension 1, may hold values from -6 to 6
- offsets: int32 [32], replicated, may hold values from 0 to 256, as said below
- taper_index: int32 [32], replicated, may hold values from 0 to 3
Outputs:
- spectral_gram: float32 [256, 64, 64], P(('group', 'tm')), parts along dimension 0
- leading_energy: float32 [256], P(('group', 'tm')), parts along dimension 0
There are 2 independent parts, one for each index of `group`. A program takes and returns all parts, laid end to end along the dimension named above; an argument that names none is the same for every part. Nothing has to cross between parts.
Inputs may be any that keep to these rules, and one draw needn't show every extreme that they name: `offsets`: block starts never fall; the first block starts at day 0 and the last at day 512 - 256.
All inputs are finite; a program needn't handle non-finite values.
Results may differ from a plain program's by a relative error of at most 0.0034.
Values may be sent and summed in bfloat16 or wider, within the bound.
A program may use at most 128 MiB of HBM per device.

v0:
```python
import math

import jax
import jax.numpy as jnp
from jax import lax
from jax.sharding import PartitionSpec as P

NFFT = 256
NB = 32
POWER = 8
NF = 128


power_eps = 1e-06


def window_rows(taper_index, length):
    steps_t = jnp.arange(length, dtype=jnp.float32)
    phase = steps_t * (2.0 * math.pi / length)
    center = (steps_t + 0.5) * (math.pi / length)
    hann = jnp.sin(center) ** 2
    hamming = 0.54 - 0.46 * jnp.cos(phase)
    blackman = 0.42 - 0.5 * jnp.cos(phase) + 0.08 * jnp.cos(2.0 * phase)
    sine_win = jnp.sin(center)
    table_rows = jnp.stack([hann, hamming, blackman, sine_win])
    chosen = jnp.zeros((taper_index.shape[0], length), jnp.float32)
    for which in range(4):
        chosen = chosen + jnp.where(
            taper_index[:, None] == which, table_rows[which][None, :], jnp.float32(0.0)
        )
    return chosen


def dft_table(length, kept):
    freqs = jnp.arange(kept, dtype=jnp.int32)
    times = jnp.arange(length, dtype=jnp.int32)
    product = freqs[:, None] * times[None, :] % length
    angle = product.astype(jnp.float32) * (2.0 * math.pi / length)
    return jnp.stack([jnp.cos(angle), -jnp.sin(angle)]).astype(jnp.bfloat16)


def local_gram(spectra):
    stacked = spectra.reshape(2 * spectra.shape[1], spectra.shape[2], spectra.shape[3])
    return jnp.einsum("ifp,jfp->fij", stacked, stacked, preferred_element_type=jnp.float32)


def shards(anomaly, offsets, taper_index):
    series = lax.all_to_all(anomaly, "tm", split_axis=1, concat_axis=0, tiled=True)
    windows = window_rows(taper_index, NFFT)
    energy = 1.0 / jnp.sqrt(jnp.sum(windows * windows, axis=1))
    transform = dft_table(NFFT, NF)
    width_here = series.shape[1]
    per_group = 8
    gram_width = 2 * NB

    def fill_group(position, buffer):
        first_block = position * per_group
        starts = lax.dynamic_slice_in_dim(offsets, first_block, per_group, 0)
        shapes = lax.dynamic_slice_in_dim(windows, first_block, per_group, 0)
        scales = lax.dynamic_slice_in_dim(energy, first_block, per_group, 0)
        segments = jax.vmap(lambda first_day: lax.dynamic_slice_in_dim(series, first_day, NFFT, 0))(
            starts
        )
        windowed = (segments * shapes[:, :, None]).astype(jnp.bfloat16)
        spectra = jnp.einsum(
            "rkt,btp->rbkp", transform, windowed, preferred_element_type=jnp.float32
        )
        spectra = (spectra * scales[None, :, None, None]).astype(jnp.bfloat16)
        return lax.dynamic_update_slice_in_dim(buffer, spectra, first_block, 1)

    empty = jnp.zeros((2, NB, NF, width_here), jnp.bfloat16)
    spectra = lax.fori_loop(0, NB // per_group, fill_group, empty)
    received = lax.all_to_all(spectra, "tm", split_axis=2, concat_axis=3, tiled=True)
    partial_value = local_gram(received)
    summed = lax.psum(partial_value, ("pix", "sub"))
    total_pixels = anomaly.shape[1] * lax.axis_size(("pix", "sub"))
    spectral_gram = summed / total_pixels
    vector = jnp.ones((spectral_gram.shape[0], gram_width), jnp.float32)
    for _ in range(POWER):
        applied = jnp.einsum("fij,fj->fi", spectral_gram, vector, precision=lax.Precision.HIGHEST)
        vector = applied / jnp.sqrt(jnp.mean(applied * applied, axis=1, keepdims=True) + power_eps)
    applied = jnp.einsum("fij,fj->fi", spectral_gram, vector, precision=lax.Precision.HIGHEST)
    leading_energy = jnp.sqrt(jnp.mean(applied * applied, axis=1))
    return (spectral_gram, leading_energy)


def solution(mesh):
    placed = (P("tm", ("group", "pix", "sub")), P(), P())
    return jax.shard_map(
        shards,
        mesh=mesh,
        in_specs=placed,
        out_specs=(P(("group", "tm"), None, None), P(("group", "tm"))),
        check_vma=False,
    )
```

profile of v0, /device:TPU:0, one launch (start us, length us, event | category | flops | bytes accessed | tf_op | source)
XLA Modules:
  0.0 1170.2 jit_solution(9330474396484308255)
XLA Ops:
  7.2 3.2 copy.48
  10.4 6.3 all-to-all-start
  18.3 47.5 %all-to-all-done = bf16[64,8,2048]{2,0,1:T(8,128)(2,1)S(1)} async-done(((bf16[64,8,2048]{2,0,1:T(8,128)(2,1)}), bf16[64,8,2048]{2,0,1:T(8,128)(2,1)S(1)}, u32[]{:S(2)}, u32[]{:S(2)}) %all-to-all-start) | async-done | bytes 2097184 | tf_op jit(solution)/shard_map/all_to_all | solution.py:48
  65.8 11.0 broadcast_in_dim.86.clone
  76.7 208.3 %while.16 = (s32[]{:T(128)}, bf16[2,32,128,2048]{3,1,0,2:T(8,128)(2,1)}, s32[32]{0:T(128)S(1)}, bf16[512,2048]{1,0:T(8,128)(2,1)S(1)}, f32[32,256]{1,0:T(8,128)S...) while((s32[]{:T(128)}, ...), condition=%wide.region_2.3_spmd, body=%wide.region_1.2_spmd.sunk | while | flops 2168455168 | bytes 52586048 | solution.py:72
  76.8 19.1 %while.17 = (s32[]{:T(128)}, bf16[512,2048]{1,0:T(8,128)(2,1)S(1)}, s32[8,2]{0,1:T(2,128)S(1)}, bf16[8,256,2048]{2,1,0:T(8,128)(2,1)}, s32[]{:T(128)}) while((s32[]{:T(128)}, bf16[512,2048]{1,0:T(8,128)(2,1)S(1)}, s32[8,2]{0,1:T(2,128)S(1)}, bf16[8,256,2048]{2,1,0:T(8,128)(2,1)}, s32[]{:T(128)}) %tuple.54), condition=%wide.while_cond, body=%wide.while_body.sunk | while | flops 2 | bytes 2098265 | solution.py:61
  77.4 1.8 bitcast_dynamic-update-slice_fusion.2
  79.7 1.9 bitcast_dynamic-update-slice_fusion.2
  82.2 1.8 bitcast_dynamic-update-slice_fusion.2
  84.5 1.8 bitcast_dynamic-update-slice_fusion.2
  86.9 1.8 bitcast_dynamic-update-slice_fusion.2
  89.3 1.8 bitcast_dynamic-update-slice_fusion.2
  91.7 1.8 bitcast_dynamic-update-slice_fusion.2
  94.1 1.8 bitcast_dynamic-update-slice_fusion.2
  96.0 12.1 %fusion.53 = bf16[2,8,128,2048]{2,3,0,1:T(8,128)(2,1)} fusion(f32[8]{0:T(128)S(1)} %dynamic_slice.28, bf16[8,256,2048]{2,1,0:T(8,128)(2,1)} %get-tuple-element.242, f32[8,256]{1,0:T(8,128)S(1)} %constant_dynamic-slice_fusion.4, bf16[2,128,256]{2,1,0:T(8,128)(2,1)S(1)} %get-tuple-element.292), kind=kOutput, calls=%fused_computation.6.clone.1 | convolution fusion | flops 2168455168 | bytes 16916512 | tf_op jit(solution)/shard_map/while/body/eval_jaxpr/rkt,btp->rbkp/dot_general | solution.py:65
  108.0 12.6 %copy.50 = bf16[2,8,128,2048]{3,1,0,2:T(8,128)(2,1)} copy(bf16[2,8,128,2048]{2,3,0,1:T(8,128)(2,1)} %fusion.53) | data formatting | bytes 16777216 | tf_op jit(solution)/shard_map/while/body/eval_jaxpr/dynamic_update_slice | solution.py:69
  120.6 8.2 constant_dynamic-update-slice_fusion.2
  128.9 19.1 %while.17 = (s32[]{:T(128)}, bf16[512,2048]{1,0:T(8,128)(2,1)S(1)}, s32[8,2]{0,1:T(2,128)S(1)}, bf16[8,256,2048]{2,1,0:T(8,128)(2,1)}, s32[]{:T(128)}) while((s32[]{:T(128)}, bf16[512,2048]{1,0:T(8,128)(2,1)S(1)}, s32[8,2]{0,1:T(2,128)S(1)}, bf16[8,256,2048]{2,1,0:T(8,128)(2,1)}, s32[]{:T(128)}) %tuple.54), condition=%wide.while_cond, body=%wide.while_body.sunk | while | flops 2 | bytes 2098265 | solution.py:61
  129.4 1.8 bitcast_dynamic-update-slice_fusion.2
  131.8 1.9 bitcast_dynamic-update-slice_fusion.2
  134.2 1.8 bitcast_dynamic-update-slice_fusion.2
  136.6 1.8 bitcast_dynamic-update-slice_fusion.2
  139.0 1.8 bitcast_dynamic-update-slice_fusion.2
  141.3 1.8 bitcast_dynamic-update-slice_fusion.2
  143.7 1.8 bitcast_dynamic-update-slice_fusion.2
  146.1 1.8 bitcast_dynamic-update-slice_fusion.2
  148.0 12.1 %fusion.53 = bf16[2,8,128,2048]{2,3,0,1:T(8,128)(2,1)} fusion(f32[8]{0:T(128)S(1)} %dynamic_slice.28, bf16[8,256,2048]{2,1,0:T(8,128)(2,1)} %get-tuple-element.242, f32[8,256]{1,0:T(8,128)S(1)} %constant_dynamic-slice_fusion.4, bf16[2,128,256]{2,1,0:T(8,128)(2,1)S(1)} %get-tuple-element.292), kind=kOutput, calls=%fused_computation.6.clone.1 | convolution fusion | flops 2168455168 | bytes 16916512 | tf_op jit(solution)/shard_map/while/body/eval_jaxpr/rkt,btp->rbkp/dot_general | solution.py:65
  160.1 12.6 %copy.50 = bf16[2,8,128,2048]{3,1,0,2:T(8,128)(2,1)} copy(bf16[2,8,128,2048]{2,3,0,1:T(8,128)(2,1)} %fusion.53) | data formatting | bytes 16777216 | tf_op jit(solution)/shard_map/while/body/eval_jaxpr/dynamic_update_slice | solution.py:69
  172.6 8.2 constant_dynamic-update-slice_fusion.2
  181.0 19.1 %while.17 = (s32[]{:T(128)}, bf16[512,2048]{1,0:T(8,128)(2,1)S(1)}, s32[8,2]{0,1:T(2,128)S(1)}, bf16[8,256,2048]{2,1,0:T(8,128)(2,1)}, s32[]{:T(128)}) while((s32[]{:T(128)}, bf16[512,2048]{1,0:T(8,128)(2,1)S(1)}, s32[8,2]{0,1:T(2,128)S(1)}, bf16[8,256,2048]{2,1,0:T(8,128)(2,1)}, s32[]{:T(128)}) %tuple.54), condition=%wide.while_cond, body=%wide.while_body.sunk | while | flops 2 | bytes 2098265 | solution.py:61
  181.5 1.8 bitcast_dynamic-update-slice_fusion.2
  183.9 1.9 bitcast_dynamic-update-slice_fusion.2
  186.3 1.8 bitcast_dynamic-update-slice_fusion.2
  188.7 1.8 bitcast_dynamic-update-slice_fusion.2
  191.1 1.8 bitcast_dynamic-update-slice_fusion.2
  193.4 1.8 bitcast_dynamic-update-slice_fusion.2
  195.8 1.8 bitcast_dynamic-update-slice_fusion.2
  198.2 1.8 bitcast_dynamic-update-slice_fusion.2
  200.1 12.1 %fusion.53 = bf16[2,8,128,2048]{2,3,0,1:T(8,128)(2,1)} fusion(f32[8]{0:T(128)S(1)} %dynamic_slice.28, bf16[8,256,2048]{2,1,0:T(8,128)(2,1)} %get-tuple-element.242, f32[8,256]{1,0:T(8,128)S(1)} %constant_dynamic-slice_fusion.4, bf16[2,128,256]{2,1,0:T(8,128)(2,1)S(1)} %get-tuple-element.292), kind=kOutput, calls=%fused_computation.6.clone.1 | convolution fusion | flops 2168455168 | bytes 16916512 | tf_op jit(solution)/shard_map/while/body/eval_jaxpr/rkt,btp->rbkp/dot_general | solution.py:65
  212.2 12.6 %copy.50 = bf16[2,8,128,2048]{3,1,0,2:T(8,128)(2,1)} copy(bf16[2,8,128,2048]{2,3,0,1:T(8,128)(2,1)} %fusion.53) | data formatting | bytes 16777216 | tf_op jit(solution)/shard_map/while/body/eval_jaxpr/dynamic_update_slice | solution.py:69
  224.7 8.2 constant_dynamic-update-slice_fusion.2
  233.0 19.1 %while.17 = (s32[]{:T(128)}, bf16[512,2048]{1,0:T(8,128)(2,1)S(1)}, s32[8,2]{0,1:T(2,128)S(1)}, bf16[8,256,2048]{2,1,0:T(8,128)(2,1)}, s32[]{:T(128)}) while((s32[]{:T(128)}, bf16[512,2048]{1,0:T(8,128)(2,1)S(1)}, s32[8,2]{0,1:T(2,128)S(1)}, bf16[8,256,2048]{2,1,0:T(8,128)(2,1)}, s32[]{:T(128)}) %tuple.54), condition=%wide.while_cond, body=%wide.while_body.sunk | while | flops 2 | bytes 2098265 | solution.py:61
  233.6 1.8 bitcast_dynamic-update-slice_fusion.2
  236.0 1.9 bitcast_dynamic-update-slice_fusion.2
  238.4 1.8 bitcast_dynamic-update-slice_fusion.2
  240.8 1.8 bitcast_dynamic-update-slice_fusion.2
  243.1 1.8 bitcast_dynamic-update-slice_fusion.2
  245.5 1.8 bitcast_dynamic-update-slice_fusion.2
  247.9 1.8 bitcast_dynamic-update-slice_fusion.2
  250.3 1.8 bitcast_dynamic-update-slice_fusion.2
  252.2 12.1 %fusion.53 = bf16[2,8,128,2048]{2,3,0,1:T(8,128)(2,1)} fusion(f32[8]{0:T(128)S(1)} %dynamic_slice.28, bf16[8,256,2048]{2,1,0:T(8,128)(2,1)} %get-tuple-element.242, f32[8,256]{1,0:T(8,128)S(1)} %constant_dynamic-slice_fusion.4, bf16[2,128,256]{2,1,0:T(8,128)(2,1)S(1)} %get-tuple-element.292), kind=kOutput, calls=%fused_computation.6.clone.1 | convolution fusion | flops 2168455168 | bytes 16916512 | tf_op jit(solution)/shard_map/while/body/eval_jaxpr/rkt,btp->rbkp/dot_general | solution.py:65
  264.2 12.6 %copy.50 = bf16[2,8,128,2048]{3,1,0,2:T(8,128)(2,1)} copy(bf16[2,8,128,2048]{2,3,0,1:T(8,128)(2,1)} %fusion.53) | data formatting | bytes 16777216 | tf_op jit(solution)/shard_map/while/body/eval_jaxpr/dynamic_update_slice | solution.py:69
  276.8 8.2 constant_dynamic-update-slice_fusion.2
  285.0 736.0 %all_to_all.34 = bf16[2,32,128,2048]{3,1,0,2:T(8,128)(2,1)} all-to-all(bf16[2,32,128,2048]{3,1,0,2:T(8,128)(2,1)} %get-tuple-element.126), channel_id=1, replica_groups=mesh['group'=2,'tm'=8,'pix'=2,'sub'=1] {'tm'}, dimensions={2} | all-to-all | bytes 67108864 | tf_op jit(solution)/shard_map/all_to_all | solution.py:73
  1021.0 30.0 %copy.21 = bf16[2,32,16,8,2048]{4,3,1,0,2:T(8,128)(2,1)} copy(bf16[2,32,16,8,2048]{4,1,0,2,3:T(8,128)(2,1)} %bitcast.107) | data formatting | bytes 67108864 | tf_op jit(solution)/shard_map/all_to_all | solution.py:73
  1051.0 49.9 %reshape.182 = bf16[64,16,16384]{2,0,1:T(8,128)(2,1)} reshape(bf16[2,32,16,8,2048]{4,3,1,0,2:T(8,128)(2,1)} %copy.21) | data formatting | bytes 67108864 | tf_op jit(solution)/shard_map/reshape | solution.py:43
  1100.9 23.5 %fusion.16 = f32[16,64,64]{2,1,0:T(8,128)} fusion(bf16[64,16,16384]{2,0,1:T(8,128)(2,1)} %reshape.182), kind=kOutput, calls=%fused_computation.64 | convolution fusion | flops 2147483648 | bytes 33816576 | tf_op jit(solution)/shard_map/ifp,jfp->fij/dot_general | solution.py:44
  1124.4 27.1 %all-reduce.3.cloned.1.call-done = f32[16,64,64]{2,1,0:T(8,128)} async-done(((f32[16,64,64]{2,1,0:T(8,128)}), f32[16,64,64]{2,1,0:T(8,128)}) %all-reduce.3.cloned.1.call-update) | async-done | bytes 262160 | tf_op jit(solution)/shard_map/psum | solution.py:75
  1151.5 1.1 broadcast_multiply_fusion
  1153.7 0.9 fusion.18
  1154.9 0.9 fusion.19
  1157.2 0.9 fusion.21
  1158.3 0.9 fusion.22
  1159.5 0.9 fusion.23
  (128 shorter events, 26.1 us)
Async XLA Ops:
  10.4 55.4 %all-to-all-start = ((bf16[64,8,2048]{2,0,1:T(8,128)(2,1)}), bf16[64,8,2048]{2,0,1:T(8,128)(2,1)S(1)}, u32[]{:S(2)}, u32[]{:S(2)}) async-start(bf16[64,8,2048]{2,0,1:T(8,128)(2,1)} %bitcast.108), calls=%async_computation | async-start | bytes 4194304 | tf_op jit(solution)/shard_map/all_to_all | solution.py:48
  16.7 1134.8 %all-reduce.3.cloned.1.call-start = ((), (), s32[]{:S(2)}) async-start(), calls=%async_computation.2 | async-start | bytes 1048576 | tf_op jit(solution)/shard_map/psum | solution.py:75
  65.7 11.0 copy-start.1
  1152.6 10.8 copy-start
Sparse Core Ops, SparseCore 0:
  1124.5 26.9 all-reduce.2
where the time goes:
time: 1170 us
  blocking collectives  736 us (63%)
  local copies, waits for them, and re-layouts  254 us (22%)
  matrix products  80.2 us (7%)
  waiting for transfers between devices  74.6 us (6%)
  between operations  14.2 us (1%)
    all_to_all x1, blocking collectives, shards(): lax.all_to_all(spectra, 'tm', split_axis=2, concat_axis=3, tiled=True)  736 us
    dynamic_update_slice x8, local copies, waits for them, and re-layouts, fill_group(): return lax.dynamic_update_slice_in_dim(buffer, spectra, first_block, 1)  83.1 us
    gather x96, local copies, waits for them, and re-layouts  76.2 us
    reshape x1, local copies, waits for them, and re-layouts, local_gram(): spectra.reshape(2 * spectra.shape[1], spectra.shape[2], spectra.shape[3])  49.9 us
    dot_general x4, matrix products, fill_group(): jnp.einsum('rkt,btp->rbkp', transform, windowed, preferred_element_type=j...  48.2 us
    all_to_all x1, waiting for transfers between devices, shards(): lax.all_to_all(anomaly, 'tm', split_axis=1, concat_axis=0, tiled=True)  47.5 us
    all_to_all x1, local copies, waits for them, and re-layouts, shards(): lax.all_to_all(spectra, 'tm', split_axis=2, concat_axis=3, tiled=True)  30 us
    psum x1, waiting for transfers between devices, shards(): summed = lax.psum(partial_value, ('pix', 'sub'))  27.1 us
  transfers between devices with their start and end apart: 2, of which 2 were waited for; matrix products, arithmetic and copies ran while one was open for 0% of the time, Pallas kernels for 0%

commit v1 on v0

v1 whole, which is shorter than its diff:
```python
import math

import jax
import jax.numpy as jnp
from jax import lax
from jax.sharding import PartitionSpec as P

NFFT = 256
NB = 32
POWER = 8
NF = 128


power_eps = 1e-06


def window_at(taper_index, steps_t, length):
    steps = steps_t.astype(jnp.float32)
    phase = steps * (2.0 * math.pi / length)
    center = (steps + 0.5) * (math.pi / length)
    hann = jnp.sin(center) ** 2
    hamming = 0.54 - 0.46 * jnp.cos(phase)
    blackman = 0.42 - 0.5 * jnp.cos(phase) + 0.08 * jnp.cos(2.0 * phase)
    sine_win = jnp.sin(center)
    which = taper_index[:, None]
    return jnp.where(
        which == 0, hann, jnp.where(which == 1, hamming, jnp.where(which == 2, blackman, sine_win))
    )


def day_operator(offsets, taper_index, freqs, days, length):
    day = jnp.arange(days, dtype=jnp.int32)
    step = day[None, :] - offsets[:, None]
    inside = (step >= 0) & (step < length)
    windows = jnp.where(inside, window_at(taper_index, step, length), 0.0)
    energy = 1.0 / jnp.sqrt(jnp.sum(windows * windows, axis=1, keepdims=True))
    scaled = windows * energy
    product = (freqs[:, None, None] * step[None]) & (length - 1)
    angle = product.astype(jnp.float32) * (2.0 * math.pi / length)
    table = jnp.stack([jnp.cos(angle), -jnp.sin(angle)], axis=1)
    table = lax.reduce_precision(table, 8, 7)
    return (table * scaled).reshape(freqs.shape[0], 2 * offsets.shape[0], days)


def shards(anomaly, offsets, taper_index):
    series = lax.all_to_all(anomaly, "tm", split_axis=1, concat_axis=0, tiled=True)
    days = series.shape[0]
    own = NF // lax.axis_size("tm")
    freqs = lax.axis_index("tm") * own + jnp.arange(own, dtype=jnp.int32)
    operator = day_operator(offsets, taper_index, freqs, days, NFFT)
    covariance = jnp.einsum("dp,ep->de", series, series, preferred_element_type=jnp.float32)
    covariance = lax.psum(covariance, ("tm", "pix", "sub"))
    total_pixels = anomaly.shape[1] * lax.axis_size(("pix", "sub"))
    half = jnp.einsum("fid,de->fie", operator, covariance, precision=lax.Precision.HIGH)
    spectral_gram = jnp.einsum("fie,fje->fij", half, operator, precision=lax.Precision.HIGH)
    spectral_gram = spectral_gram / total_pixels
    vector = jnp.ones((own, 2 * NB), jnp.float32)
    for _ in range(POWER):
        applied = jnp.einsum("fij,fj->fi", spectral_gram, vector, precision=lax.Precision.HIGHEST)
        vector = applied / jnp.sqrt(jnp.mean(applied * applied, axis=1, keepdims=True) + power_eps)
    applied = jnp.einsum("fij,fj->fi", spectral_gram, vector, precision=lax.Precision.HIGHEST)
    leading_energy = jnp.sqrt(jnp.mean(applied * applied, axis=1))
    return (spectral_gram, leading_energy)


def solution(mesh):
    placed = (P("tm", ("group", "pix", "sub")), P(), P())
    return jax.shard_map(
        shards,
        mesh=mesh,
        in_specs=placed,
        out_specs=(P(("group", "tm"), None, None), P(("group", "tm"))),
        check_vma=False,
    )
```

time: 1170 us -> 185 us (0.16)
  blocking collectives: 736 us -> 0 us
  local copies, waits for them, and re-layouts: 254 us -> 3.17 us
  matrix products: 80.2 us -> 17.3 us
  waiting for transfers between devices: 74.6 us -> 135 us
    all_to_all x1 -> x0, blocking collectives: 736 us -> none  [shards(): lax.all_to_all(spectra, 'tm', split_axis=2, concat_axis=3, tiled=True)]
    dynamic_update_slice x8 -> x0, local copies, waits for them, and re-layouts: 83.1 us -> none  [fill_group(): return lax.dynamic_update_slice_in_dim(buffer, spectra, first_block, 1)]
    gather x96 -> x0, local copies, waits for them, and re-layouts: 76.2 us -> none
    psum x1, waiting for transfers between devices: 27.1 us -> 90.9 us  [shards(): covariance = lax.psum(covariance, ('tm', 'pix', 'sub'))]
    dot_general x5 -> x3, matrix products: 71.7 us -> 8.66 us  [the longest x1 4.49 us: shards(): jnp.einsum('dp,ep->de', series, series, preferred_element_type=jnp.float32)]
    reshape x1 -> x0, local copies, waits for them, and re-layouts: 49.9 us -> none  [local_gram(): spectra.reshape(2 * spectra.shape[1], spectra.shape[2], spectra.shape[3])]
    all_to_all x1 -> x0, local copies, waits for them, and re-layouts: 30 us -> none  [shards(): lax.all_to_all(spectra, 'tm', split_axis=2, concat_axis=3, tiled=True)]
  transfers between devices with their start and end apart: 2 -> 2, of which waited for: 2 -> 2; matrix products, arithmetic and copies ran while one was open for 0% -> 3% of each run, Pallas kernels for 0% -> 0%
where the time goes in v1:
time: 185 us
  waiting for transfers between devices  135 us (73%)
  matrix products  17.3 us (9%)
  between operations  14.2 us (8%)
  other arithmetic  8.3 us (4%)
  starting transfers between devices  6.49 us (4%)
  local copies, waits for them, and re-layouts  3.17 us (2%)
    psum x1, waiting for transfers between devices, shards(): covariance = lax.psum(covariance, ('tm', 'pix', 'sub'))  90.9 us
    all_to_all x1, waiting for transfers between devices, shards(): lax.all_to_all(anomaly, 'tm', split_axis=1, concat_axis=0, tiled=True)  44.3 us
    dot_general x9, matrix products, shards(): jnp.einsum('fij,fj->fi', spectral_gram, vector, precision=lax.Precision.H...  8.59 us
    all_to_all x1, starting transfers between devices, shards(): lax.all_to_all(anomaly, 'tm', split_axis=1, concat_axis=0, tiled=True)  6.46 us
    dot_general x1, matrix products, shards(): jnp.einsum('dp,ep->de', series, series, preferred_element_type=jnp.float32)  4.49 us
    cos x1, other arithmetic, day_operator(): table = jnp.stack([jnp.cos(angle), -jnp.sin(angle)], axis=1)  3.82 us
  transfers between devices with their start and end apart: 2, of which 2 were waited for; matrix products, arithmetic and copies ran while one was open for 3% of the time, Pallas kernels for 0%

profile of v1, /device:TPU:0, one launch (start us, length us, event | category | flops | bytes accessed | tf_op | source)
XLA Modules:
  0.0 184.7 jit_solution(9127771249241529888)
XLA Ops:
  7.2 3.1 %copy.28 = bf16[8,8,8,2048]{3,2,0,1:T(8,128)(2,1)} copy(bf16[8,8,8,2048]{3,2,1,0:T(8,128)(2,1)} %bitcast.79) | data formatting | bytes 4194304 | tf_op jit(solution)/shard_map/all_to_all | solution.py:46
  10.3 0.0 copy-start.2
  10.3 0.0 copy-start.1
  10.3 6.5 %all-to-all-start = ((bf16[64,8,2048]{2,0,1:T(8,128)(2,1)}), bf16[64,8,2048]{2,0,1:T(8,128)(2,1)}, u32[]{:S(2)}, u32[]{:S(2)}) async-start(bf16[64,8,2048]{2,0,1:T(8,128)(2,1)} %bitcast.78), calls=%async_computation | async-start | bytes 4194304 | tf_op jit(solution)/shard_map/all_to_all | solution.py:46
  16.8 0.0 all-reduce.2.cloned.1.call-start
  16.8 0.0 copy-done.2
  16.8 0.0 copy-done.1
  16.8 0.9 multiply_reduce_fusion
  17.7 0.1 iota_subtract_fusion
  17.8 3.8 %fusion.2 = (f32[16,1,32,512]{3,2,1,0:T(8,128)S(1)}, f32[16,1,32,512]{3,2,1,0:T(8,128)S(1)}) fusion(s32[32,512]{1,0:T(8,128)S(1)} %iota_subtract_fusion, s32[16]{0:T(128)S(1)} %iota_add_fusion), kind=kLoop, calls=%fused_computation.8 | loop fusion | flops 1310720 | bytes 2162752 | tf_op jit(solution)/shard_map/cos | solution.py:40
  21.6 44.3 %all-to-all-done = bf16[64,8,2048]{2,0,1:T(8,128)(2,1)} async-done(((bf16[64,8,2048]{2,0,1:T(8,128)(2,1)}), bf16[64,8,2048]{2,0,1:T(8,128)(2,1)}, u32[]{:S(2)}, u32[]{:S(2)}) %all-to-all-start) | async-done | bytes 2097184 | tf_op jit(solution)/shard_map/all_to_all | solution.py:46
  65.9 4.5 %fusion.6 = f32[512,512]{1,0:T(8,128)} fusion(bf16[512,2048]{1,0:T(8,128)(2,1)} %bitcast.3), kind=kOutput, calls=%fused_computation.46 | convolution fusion | flops 1073741824 | bytes 3145728 | tf_op jit(solution)/shard_map/dp,ep->de/dot_general | solution.py:51
  70.4 0.0 all-reduce.2.cloned.1.call-update
  70.4 0.8 broadcast_multiply_fusion
  71.2 0.2 maximum_reduce-precision_fusion
  71.5 0.3 bitcast_multiply_fusion
  71.8 90.9 %all-reduce.2.cloned.1.call-done = f32[512,512]{1,0:T(8,128)} async-done(((f32[512,512]{1,0:T(8,128)}), f32[512,512]{1,0:T(8,128)}) %all-reduce.2.cloned.1.call-update) | async-done | bytes 1048592 | tf_op jit(solution)/shard_map/psum | solution.py:52
  162.7 3.0 %fusion = f32[16,64,512]{2,1,0:T(8,128)S(1)} fusion(f32[16,64,512]{2,1,0:T(8,128)S(1)} %bitcast_multiply_fusion, f32[512,512]{1,0:T(8,128)} %all-reduce.2.cloned.1.call-done), kind=kOutput, calls=%fused_computation.4 | convolution fusion | flops 1610612736 | bytes 5242880 | tf_op jit(solution)/shard_map/fid,de->fie/dot_general | solution.py:54
  165.7 1.1 convolution_multiply_fusion
  166.8 0.0 copy-start
  166.9 0.9 fusion.7
  167.8 0.1 multiply_reduce_fusion.9
  167.9 0.1 broadcast_divide_fusion.7
  168.0 0.9 fusion.8
  168.9 0.1 multiply_reduce_fusion.8
  169.1 0.1 broadcast_divide_fusion.6
  169.2 0.9 fusion.9
  170.1 0.1 multiply_reduce_fusion.7
  170.2 0.1 broadcast_divide_fusion.5
  170.3 1.1 fusion.10
  171.4 0.1 multiply_reduce_fusion.6
  171.6 0.1 broadcast_divide_fusion.4
  171.6 0.9 fusion.11
  172.6 0.1 multiply_reduce_fusion.5
  172.7 0.1 broadcast_divide_fusion.3
  172.8 0.9 fusion.12
  173.7 0.1 multiply_reduce_fusion.4
  173.9 0.1 broadcast_divide_fusion.2
  173.9 0.9 fusion.13
  174.9 0.1 multiply_reduce_fusion.3
  175.0 0.1 broadcast_divide_fusion.1
  175.1 0.9 fusion.14
  176.0 0.1 multiply_reduce_fusion.2
  176.2 0.1 broadcast_divide_fusion
  176.2 0.0 copy-done
  176.2 0.9 fusion.15
  177.2 0.1 multiply_reduce_fusion.1
  177.3 0.5 multiply_sqrt_fusion
  (13 shorter events, 0.1 us)
Async XLA Ops:
  10.3 6.5 %copy-start.2 = (s32[32]{0:T(128)S(1)}, s32[32]{0:T(128)}, u32[]{:S(2)}) copy-start(s32[32]{0:T(128)} %param.5) | copy-start | bytes 388
  10.3 6.5 %copy-start.1 = (s32[32]{0:T(128)S(1)}, s32[32]{0:T(128)}, u32[]{:S(2)}) copy-start(s32[32]{0:T(128)} %param.4) | copy-start | bytes 388
  10.3 55.6 %all-to-all-start = ((bf16[64,8,2048]{2,0,1:T(8,128)(2,1)}), bf16[64,8,2048]{2,0,1:T(8,128)(2,1)}, u32[]{:S(2)}, u32[]{:S(2)}) async-start(bf16[64,8,2048]{2,0,1:T(8,128)(2,1)} %bitcast.78), calls=%async_computation | async-start | bytes 4194304 | tf_op jit(solution)/shard_map/all_to_all | solution.py:46
  16.8 145.9 %all-reduce.2.cloned.1.call-start = ((), (), s32[]{:S(2)}) async-start(), calls=%async_computation.1 | async-start | bytes 2097152 | tf_op jit(solution)/shard_map/psum | solution.py:52
  166.8 9.4 %copy-start = (f32[16,64,64]{2,1,0:T(8,128)}, f32[16,64,64]{2,1,0:T(8,128)S(1)}, u32[]{:S(2)}) copy-start(f32[16,64,64]{2,1,0:T(8,128)S(1)} %convolution_multiply_fusion) | copy-start | bytes 786436
Sparse Core Ops, SparseCore 0:
  70.6 92.0 all-reduce.1

commit v2 on v1

--- a/solution.py
+++ b/solution.py
@@ -1,8 +1,11 @@
+import functools
 import math
 
 import jax
 import jax.numpy as jnp
 from jax import lax
+from jax.experimental import pallas as pl
+from jax.experimental.pallas import tpu as pltpu
 from jax.sharding import PartitionSpec as P
 
 NFFT = 256
@@ -42,25 +45,175 @@
     return (table * scaled).reshape(freqs.shape[0], 2 * offsets.shape[0], days)
 
 
+BLOCK = 128
+MESH = pl.DeviceIdType.MESH
+
+
+def stages_of(tm, pix, sub):
+    if sub > 1 or tm % 2:
+        split = [("sub", 1, sub), ("pix", 1, pix), ("tm", 1, tm)]
+    else:
+        split = [("tm", 1, 2), ("pix", 1, pix), ("tm", 2, tm // 2)]
+    return [stage for stage in split if stage[2] > 1]
+
+
+def place_in(stage):
+    axis, inner, members = stage
+    return lax.rem(lax.axis_index(axis) // inner, members)
+
+
+def device_at(stage, shift):
+    axis, inner, members = stage
+    index = lax.axis_index(axis)
+    here = place_in(stage)
+    there = lax.rem(here + shift, members)
+    return {axis: index + (there - here) * inner}, there
+
+
+def covariance_kernel(stages, series, out, packed, gathered, *scratch):
+    count = len(stages)
+    landing = scratch[:count]
+    sems = scratch[count:]
+    days = series.shape[0]
+    blocks = days // BLOCK
+
+    barrier = pltpu.get_barrier_semaphore()
+    for stage in stages:
+        for shift in range(1, stage[2]):
+            pl.semaphore_signal(barrier, inc=1, device_id=device_at(stage, shift)[0], device_id_type=MESH)
+
+    place = 0
+    for i in range(blocks):
+        strip = lax.dot_general(
+            series[i * BLOCK : (i + 1) * BLOCK, :],
+            series[i * BLOCK :, :],
+            (((1,), (1,)), ((), ())),
+            preferred_element_type=jnp.float32,
+        )
+        for j in range(blocks - i):
+            packed[pl.ds((place + j) * BLOCK, BLOCK), :] = strip[:, j * BLOCK : (j + 1) * BLOCK]
+        place += blocks - i
+    if packed.shape[0] > place * BLOCK:
+        packed[place * BLOCK :, :] = jnp.zeros((packed.shape[0] - place * BLOCK, BLOCK), jnp.float32)
+    pl.semaphore_wait(barrier, sum(stage[2] - 1 for stage in stages))
+
+    start, rows = 0, packed.shape[0]
+    starts = []
+    for s, stage in enumerate(stages):
+        members = stage[2]
+        part = rows // members
+        starts.append(start)
+        copies = []
+        for shift in range(1, members):
+            device, there = device_at(stage, shift)
+            copy = pltpu.make_async_remote_copy(
+                src_ref=packed.at[pl.ds(pl.multiple_of(start + there * part, 8), part), :],
+                dst_ref=landing[s].at[shift - 1],
+                send_sem=sems[4 * s].at[shift - 1],
+                recv_sem=sems[4 * s + 1].at[shift - 1],
+                device_id=device,
+                device_id_type=MESH,
+            )
+            copy.start()
+            copies.append(copy)
+        start = start + place_in(stage) * part
+        rows = part
+        own = packed.at[pl.ds(pl.multiple_of(start, 8), part), :]
+        total = own[...]
+        for shift in range(1, members):
+            copies[shift - 1].wait()
+            total = total + landing[s][shift - 1]
+        own[...] = total
+    gathered[pl.ds(pl.multiple_of(start, 8), rows), :] = total
+
+    for s in reversed(range(count)):
+        stage = stages[s]
+        own = gathered.at[pl.ds(pl.multiple_of(start, 8), rows), :]
+        copies = []
+        for shift in range(1, stage[2]):
+            copy = pltpu.make_async_remote_copy(
+                src_ref=own,
+                dst_ref=own,
+                send_sem=sems[4 * s + 2].at[shift - 1],
+                recv_sem=sems[4 * s + 3].at[shift - 1],
+                device_id=device_at(stage, shift)[0],
+                device_id_type=MESH,
+            )
+            copy.start()
+            copies.append(copy)
+        for copy in copies:
+            copy.wait()
+        start, rows = starts[s], rows * stage[2]
+
+    place = 0
+    for i in range(blocks):
+        for j in range(i, blocks):
+            block = gathered[pl.ds(place * BLOCK, BLOCK), :]
+            out[pl.ds(i * BLOCK, BLOCK), pl.ds(j * BLOCK, BLOCK)] = block
+            if j > i:
+                out[pl.ds(j * BLOCK, BLOCK), pl.ds(i * BLOCK, BLOCK)] = block.T
+            place += 1
+
+
+def summed_covariance(series):
+    days = series.shape[0]
+    stages = stages_of(lax.axis_size("tm"), lax.axis_size("pix"), lax.axis_size("sub"))
+    devices = math.prod(stage[2] for stage in stages)
+    blocks = days // BLOCK
+    rows = -(-(blocks * (blocks + 1) // 2 * BLOCK) // (8 * devices)) * 8 * devices
+    landing, sems, part = [], [], rows
+    for stage in stages:
+        part //= stage[2]
+        landing.append(pltpu.VMEM((stage[2] - 1, part, BLOCK), jnp.float32))
+        sems += [pltpu.SemaphoreType.DMA((stage[2] - 1,))] * 4
+    return pl.pallas_call(
+        functools.partial(covariance_kernel, stages),
+        out_shape=jax.ShapeDtypeStruct((days, days), jnp.float32),
+        in_specs=[pl.BlockSpec(memory_space=pltpu.VMEM)],
+        out_specs=pl.BlockSpec(memory_space=pltpu.VMEM),
+        scratch_shapes=[pltpu.VMEM((rows, BLOCK), jnp.float32)] * 2 + landing + sems,
+        compiler_params=pltpu.CompilerParams(
+            collective_id=0, has_side_effects=True, vmem_limit_bytes=48 * 2**20
+        ),
+        name="covariance",
+    )(series)
+
+
+def leading_kernel(gram_ref, lead_ref):
+    gram = gram_ref[...]
+    size = gram.shape[1]
+    vector = jnp.ones((gram.shape[0], 1, size), jnp.float32)
+    for step in range(POWER + 1):
+        across = 2 - step % 2
+        applied = jnp.sum(gram * vector, axis=across, keepdims=True)
+        power = jnp.sum(applied * applied, axis=3 - across, keepdims=True) / size
+        vector = applied / jnp.sqrt(power + power_eps)
+    lead_ref[...] = jnp.broadcast_to(jnp.sqrt(power)[:, 0, :], lead_ref.shape)
+
+
+def leading_mode(spectral_gram):
+    own = spectral_gram.shape[0]
+    lead = pl.pallas_call(
+        leading_kernel,
+        out_shape=jax.ShapeDtypeStruct((own, BLOCK), jnp.float32),
+        in_specs=[pl.BlockSpec(memory_space=pltpu.VMEM)],
+        out_specs=pl.BlockSpec(memory_space=pltpu.VMEM),
+        name="leading",
+    )(spectral_gram)
+    return lead[:, 0]
+
+
 def shards(anomaly, offsets, taper_index):
     series = lax.all_to_all(anomaly, "tm", split_axis=1, concat_axis=0, tiled=True)
-    days = series.shape[0]
     own = NF // lax.axis_size("tm")
     freqs = lax.axis_index("tm") * own + jnp.arange(own, dtype=jnp.int32)
-    operator = day_operator(offsets, taper_index, freqs, days, NFFT)
-    covariance = jnp.einsum("dp,ep->de", series, series, preferred_element_type=jnp.float32)
-    covariance = lax.psum(covariance, ("tm", "pix", "sub"))
     total_pixels = anomaly.shape[1] * lax.axis_size(("pix", "sub"))
+    operator = day_operator(offsets, taper_index, freqs, series.shape[0], NFFT)
+    covariance = summed_covariance(series)
     half = jnp.einsum("fid,de->fie", operator, covariance, precision=lax.Precision.HIGH)
     spectral_gram = jnp.einsum("fie,fje->fij", half, operator, precision=lax.Precision.HIGH)
     spectral_gram = spectral_gram / total_pixels
-    vector = jnp.ones((own, 2 * NB), jnp.float32)
-    for _ in range(POWER):
-        applied = jnp.einsum("fij,fj->fi", spectral_gram, vector, precision=lax.Precision.HIGHEST)
-        vector = applied / jnp.sqrt(jnp.mean(applied * applied, axis=1, keepdims=True) + power_eps)
-    applied = jnp.einsum("fij,fj->fi", spectral_gram, vector, precision=lax.Precision.HIGHEST)
-    leading_energy = jnp.sqrt(jnp.mean(applied * applied, axis=1))
-    return (spectral_gram, leading_energy)
+    return (spectral_gram, leading_mode(spectral_gram))
 
 
 def solution(mesh):

time: 185 us -> 91.4 us (0.49)
  waiting for transfers between devices: 135 us -> 41.5 us
  Pallas kernels: 0 us -> 26.8 us
  matrix products: 17.3 us -> 3.66 us
  between operations: 14.2 us -> 0.72 us
    psum x1 -> x0, waiting for transfers between devices: 90.9 us -> none  [shards(): covariance = lax.psum(covariance, ('tm', 'pix', 'sub'))]
    pallas_call x0 -> x2, Pallas kernels: none -> 26.8 us  [the longest x1 23.8 us: summed_covariance(): pl.pallas_call(functools.partial(covariance_kernel, stages), out_shape=ja...]
    dot_general x10 -> x0, matrix products: 13.1 us -> none  [the longest x9 8.59 us: shards(): jnp.einsum('fij,fj->fi', spectral_gram, vector, precision=lax.Precision.H...]
    all_to_all x1, waiting for transfers between devices: 44.3 us -> 41.5 us  [shards(): lax.all_to_all(anomaly, 'tm', split_axis=1, concat_axis=0, tiled=True)]
  transfers between devices with their start and end apart: 2 -> 1, of which waited for: 2 -> 1; matrix products, arithmetic and copies ran while one was open for 3% -> 8% of each run, Pallas kernels for 0% -> 0%
where the time goes in v2:
time: 91.4 us; the launch traced here: 91.1 us
  waiting for transfers between devices  41.5 us (45%)
  Pallas kernels  26.8 us (29%)
  other arithmetic  7.53 us (8%)
  starting transfers between devices  6.46 us (7%)
  local copies, waits for them, and re-layouts  4.49 us (5%)
  matrix products  3.66 us (4%)
    all_to_all x1, waiting for transfers between devices, shards(): lax.all_to_all(anomaly, 'tm', split_axis=1, concat_axis=0, tiled=True)  41.5 us
    pallas_call x1, Pallas kernels, summed_covariance(): pl.pallas_call(functools.partial(covariance_kernel, stages), out_shape=ja...  23.8 us
    all_to_all x1, starting transfers between devices, shards(): lax.all_to_all(anomaly, 'tm', split_axis=1, concat_axis=0, tiled=True)  6.46 us
    cos x1, other arithmetic, day_operator(): table = jnp.stack([jnp.cos(angle), -jnp.sin(angle)], axis=1)  3.82 us
    all_to_all x1, local copies, waits for them, and re-layouts, shards(): lax.all_to_all(anomaly, 'tm', split_axis=1, concat_axis=0, tiled=True)  3.14 us
    pallas_call x1, Pallas kernels, leading_mode(): pl.pallas_call(leading_kernel, out_shape=jax.ShapeDtypeStruct((own, BLOCK...  2.94 us
    dot_general x1, matrix products, shards(): jnp.einsum('fie,fje->fij', half, operator, precision=lax.Precision.HIGH)  1.85 us
  transfers between devices with their start and end apart: 1, of which 1 were waited for; matrix products, arithmetic and copies ran while one was open for 8% of the time, Pallas kernels for 0%

profile of v2, /device:TPU:0, one launch (start us, length us, event | category | flops | bytes accessed | tf_op | source)
XLA Modules:
  0.0 91.1 jit_solution(3414109924102617140)
XLA Ops:
  0.6 3.1 %copy.9 = bf16[8,8,8,2048]{3,2,0,1:T(8,128)(2,1)} copy(bf16[8,8,8,2048]{3,2,1,0:T(8,128)(2,1)} %bitcast.18) | data formatting | bytes 4194304 | tf_op jit(solution)/shard_map/all_to_all | solution.py:207
  3.8 0.0 copy-start.2
  3.8 0.0 copy-start.1
  3.8 6.5 %all-to-all-start = ((bf16[64,8,2048]{2,0,1:T(8,128)(2,1)}), bf16[64,8,2048]{2,0,1:T(8,128)(2,1)S(1)}, u32[]{:S(2)}, u32[]{:S(2)}) async-start(bf16[64,8,2048]{2,0,1:T(8,128)(2,1)} %bitcast.17), calls=%async_computation | async-start | bytes 4194304 | tf_op jit(solution)/shard_map/all_to_all | solution.py:207
  10.2 0.0 copy-done.2
  10.3 0.0 copy-done.1
  10.3 0.9 multiply_reduce_fusion
  11.1 0.1 iota_subtract_fusion
  11.2 3.8 %fusion.2 = (f32[16,1,32,512]{3,2,1,0:T(8,128)S(1)}, f32[16,1,32,512]{3,2,1,0:T(8,128)S(1)}) fusion(s32[32,512]{1,0:T(8,128)S(1)} %iota_subtract_fusion, s32[16]{0:T(128)S(1)} %iota_add_fusion), kind=kLoop, calls=%fused_computation.8 | loop fusion | flops 1310720 | bytes 2162752 | tf_op jit(solution)/shard_map/cos | solution.py:43
  15.0 0.3 maximum_reduce-precision_fusion
  15.4 0.8 broadcast_multiply_fusion
  16.2 1.7 %bitcast_multiply_fusion = f32[16,64,512]{2,1,0:T(8,128)} fusion(f32[16,2,32,512]{3,2,1,0:T(8,128)S(1)} %maximum_reduce-precision_fusion, f32[64,512]{1,0:T(8,128)S(1)} %bitcast.19), kind=kLoop, calls=%fused_computation.2 | loop fusion | flops 524288 | bytes 4325376 | tf_op jit(solution)/shard_map/mul | solution.py:45
  17.8 41.5 %all-to-all-done = bf16[64,8,2048]{2,0,1:T(8,128)(2,1)S(1)} async-done(((bf16[64,8,2048]{2,0,1:T(8,128)(2,1)}), bf16[64,8,2048]{2,0,1:T(8,128)(2,1)S(1)}, u32[]{:S(2)}, u32[]{:S(2)}) %all-to-all-start) | async-done | bytes 2097184 | tf_op jit(solution)/shard_map/all_to_all | solution.py:207
  59.3 0.0 copy-start
  59.3 23.8 %covariance.1 = f32[512,512]{1,0:T(8,128)S(1)} custom-call(bf16[512,2048]{1,0:T(8,128)(2,1)S(1)} %bitcast.16), custom_call_target="tpu_custom_call" | custom-call | tf_op jit(solution)/shard_map/covariance/pallas_call | solution.py:169
  83.1 0.0 copy-done
  83.1 1.8 %fusion = f32[16,64,512]{2,1,0:T(8,128)S(1)} fusion(f32[16,64,512]{2,1,0:T(8,128)S(1)} %copy-done, f32[512,512]{1,0:T(8,128)S(1)} %covariance.1), kind=kOutput, calls=%fused_computation.4 | convolution fusion | flops 1610612736 | bytes 5242880 | tf_op jit(solution)/shard_map/fid,de->fie/dot_general | solution.py:213
  85.0 1.8 %convolution_multiply_fusion.gram_ref = f32[16,64,64]{2,1,0:T(8,128)} fusion(f32[16,64,512]{2,1,0:T(8,128)S(1)} %fusion, f32[16,64,512]{2,1,0:T(8,128)S(1)} %copy-done), kind=kOutput, calls=%fused_computation.3 | convolution fusion | flops 201392128 | bytes 4456448 | tf_op jit(solution)/shard_map/fie,fje->fij/dot_general | solution.py:214
  86.8 2.9 %leading.1 = f32[16,128]{1,0:T(8,128)} custom-call(f32[16,64,64]{2,1,0:T(8,128)} %convolution_multiply_fusion.gram_ref), custom_call_target="tpu_custom_call" | custom-call | tf_op jit(solution)/shard_map/leading/pallas_call | solution.py:196
  89.7 1.3 %slice_reduce_fusion = f32[16]{0:T(128)} fusion(f32[16,128]{1,0:T(8,128)} %leading.1), kind=kLoop, calls=%fused_computation.16 | loop fusion | bytes 128 | tf_op jit(solution)/shard_map/slice | solution.py:203
  (4 shorter events, 0.0 us)
Async XLA Ops:
  3.8 6.5 %copy-start.2 = (s32[32]{0:T(128)S(1)}, s32[32]{0:T(128)}, u32[]{:S(2)}) copy-start(s32[32]{0:T(128)} %param.5) | copy-start | bytes 388
  3.8 6.5 %copy-start.1 = (s32[32]{0:T(128)S(1)}, s32[32]{0:T(128)}, u32[]{:S(2)}) copy-start(s32[32]{0:T(128)} %param.4) | copy-start | bytes 388
  3.8 55.5 %all-to-all-start = ((bf16[64,8,2048]{2,0,1:T(8,128)(2,1)}), bf16[64,8,2048]{2,0,1:T(8,128)(2,1)S(1)}, u32[]{:S(2)}, u32[]{:S(2)}) async-start(bf16[64,8,2048]{2,0,1:T(8,128)(2,1)} %bitcast.17), calls=%async_computation | async-start | bytes 4194304 | tf_op jit(solution)/shard_map/all_to_all | solution.py:207
  59.3 23.8 %copy-start = (f32[16,64,512]{2,1,0:T(8,128)S(1)}, f32[16,64,512]{2,1,0:T(8,128)}, u32[]{:S(2)}) copy-start(f32[16,64,512]{2,1,0:T(8,128)} %bitcast_multiply_fusion) | copy-start | bytes 6291460

commit v3 on v2

--- a/solution.py
+++ b/solution.py
@@ -17,32 +17,37 @@
 power_eps = 1e-06
 
 
-def window_at(taper_index, steps_t, length):
-    steps = steps_t.astype(jnp.float32)
+CHUNKS = 4
+
+
+def windows_of(taper, step, length):
+    steps = step.astype(jnp.float32)
     phase = steps * (2.0 * math.pi / length)
     center = (steps + 0.5) * (math.pi / length)
-    hann = jnp.sin(center) ** 2
+    sine_win = jnp.sin(center)
+    hann = sine_win * sine_win
     hamming = 0.54 - 0.46 * jnp.cos(phase)
     blackman = 0.42 - 0.5 * jnp.cos(phase) + 0.08 * jnp.cos(2.0 * phase)
-    sine_win = jnp.sin(center)
-    which = taper_index[:, None]
-    return jnp.where(
-        which == 0, hann, jnp.where(which == 1, hamming, jnp.where(which == 2, blackman, sine_win))
+    chosen = jnp.where(
+        taper == 0, hann, jnp.where(taper == 1, hamming, jnp.where(taper == 2, blackman, sine_win))
     )
-
-
-def day_operator(offsets, taper_index, freqs, days, length):
-    day = jnp.arange(days, dtype=jnp.int32)
-    step = day[None, :] - offsets[:, None]
-    inside = (step >= 0) & (step < length)
-    windows = jnp.where(inside, window_at(taper_index, step, length), 0.0)
-    energy = 1.0 / jnp.sqrt(jnp.sum(windows * windows, axis=1, keepdims=True))
-    scaled = windows * energy
-    product = (freqs[:, None, None] * step[None]) & (length - 1)
-    angle = product.astype(jnp.float32) * (2.0 * math.pi / length)
-    table = jnp.stack([jnp.cos(angle), -jnp.sin(angle)], axis=1)
-    table = lax.reduce_precision(table, 8, 7)
-    return (table * scaled).reshape(freqs.shape[0], 2 * offsets.shape[0], days)
+    return jnp.where((step >= 0) & (step < length), chosen, 0.0)
+
+
+def write_operator(offsets, taper, operator):
+    own, _, days = operator.shape
+    step = lax.broadcasted_iota(jnp.int32, (NB, days), 1) - offsets[...]
+    windows = windows_of(jnp.broadcast_to(taper[...], (NB, days)), step, NFFT)
+    scaled = windows * (1.0 / jnp.sqrt(jnp.sum(windows * windows, axis=1, keepdims=True)))
+    first = lax.axis_index("tm") * own
+
+    def one(f, carry):
+        angle = (((first + f) * step) & (NFFT - 1)).astype(jnp.float32) * (2.0 * math.pi / NFFT)
+        operator[f, :NB, :] = jnp.cos(angle).astype(jnp.bfloat16).astype(jnp.float32) * scaled
+        operator[f, NB:, :] = (-jnp.sin(angle)).astype(jnp.bfloat16).astype(jnp.float32) * scaled
+        return carry
+
+    lax.fori_loop(0, own, one, 0)
 
 
 BLOCK = 128
@@ -70,18 +75,8 @@
     return {axis: index + (there - here) * inner}, there
 
 
-def covariance_kernel(stages, series, out, packed, gathered, *scratch):
-    count = len(stages)
-    landing = scratch[:count]
-    sems = scratch[count:]
-    days = series.shape[0]
-    blocks = days // BLOCK
-
-    barrier = pltpu.get_barrier_semaphore()
-    for stage in stages:
-        for shift in range(1, stage[2]):
-            pl.semaphore_signal(barrier, inc=1, device_id=device_at(stage, shift)[0], device_id_type=MESH)
-
+def add_products(series, packed, first):
+    blocks = series.shape[0] // BLOCK
     place = 0
     for i in range(blocks):
         strip = lax.dot_general(
@@ -91,11 +86,73 @@
             preferred_element_type=jnp.float32,
         )
         for j in range(blocks - i):
-            packed[pl.ds((place + j) * BLOCK, BLOCK), :] = strip[:, j * BLOCK : (j + 1) * BLOCK]
+            rows = pl.ds((place + j) * BLOCK, BLOCK)
+            block = strip[:, j * BLOCK : (j + 1) * BLOCK]
+            packed[rows, :] = block if first else packed[rows, :] + block
         place += blocks - i
-    if packed.shape[0] > place * BLOCK:
-        packed[place * BLOCK :, :] = jnp.zeros((packed.shape[0] - place * BLOCK, BLOCK), jnp.float32)
-    pl.semaphore_wait(barrier, sum(stage[2] - 1 for stage in stages))
+
+
+def covariance_kernel(
+    stages, anomaly, offsets, taper, out, operator, series, packed, gathered, own_sem, *scratch
+):
+    exchange_send, exchange_recv = scratch[:2]
+    count = len(stages)
+    landing = scratch[2 : 2 + count]
+    sems = scratch[2 + count :]
+    chunks, days, width = series.shape
+    per_device = anomaly.shape[0]
+    peers = days // per_device
+    me = lax.axis_index("tm")
+
+    barrier = pltpu.get_barrier_semaphore()
+    greeted = 0
+    for axis in ("tm", "pix", "sub"):
+        members = lax.axis_size(axis)
+        for shift in range(1, members):
+            device = {axis: lax.rem(lax.axis_index(axis) + shift, members)}
+            pl.semaphore_signal(barrier, inc=1, device_id=device, device_id_type=MESH)
+            greeted += 1
+    my_rows = pl.ds(pl.multiple_of(me * per_device, per_device), per_device)
+
+    def columns(device, chunk):
+        return pl.ds(pl.multiple_of(device * (chunks * width) + chunk * width, width), width)
+
+    kept = []
+    for chunk in range(chunks):
+        copy = pltpu.make_async_copy(
+            anomaly.at[:, columns(me, chunk)], series.at[chunk, my_rows, :], own_sem.at[chunk]
+        )
+        copy.start()
+        kept.append(copy)
+    pl.semaphore_wait(barrier, greeted)
+    farthest_first = sorted(range(1, peers), key=lambda shift: abs(2 * shift - peers))
+    exchanged = []
+    for chunk in range(chunks):
+        copies = []
+        for shift in farthest_first:
+            there = lax.rem(me + shift, peers)
+            copy = pltpu.make_async_remote_copy(
+                src_ref=anomaly.at[:, columns(there, chunk)],
+                dst_ref=series.at[chunk, my_rows, :],
+                send_sem=exchange_send.at[chunk, shift - 1],
+                recv_sem=exchange_recv.at[chunk, shift - 1],
+                device_id={"tm": there},
+                device_id_type=MESH,
+            )
+            copy.start()
+            copies.append(copy)
+        exchanged.append(copies)
+
+    write_operator(offsets, taper, operator)
+    blocks = days // BLOCK
+    filled = blocks * (blocks + 1) // 2 * BLOCK
+    if packed.shape[0] > filled:
+        packed[filled:, :] = jnp.zeros((packed.shape[0] - filled, BLOCK), jnp.float32)
+    for chunk in range(chunks):
+        kept[chunk].wait()
+        for copy in exchanged[chunk]:
+            copy.wait()
+        add_products(series.at[chunk], packed, chunk == 0)
 
     start, rows = 0, packed.shape[0]
     starts = []
@@ -155,9 +212,12 @@
             place += 1
 
 
-def summed_covariance(series):
-    days = series.shape[0]
-    stages = stages_of(lax.axis_size("tm"), lax.axis_size("pix"), lax.axis_size("sub"))
+def covariance_and_operator(anomaly, offsets, taper_index):
+    per_device, pixels = anomaly.shape
+    peers = lax.axis_size("tm")
+    days = per_device * peers
+    own = NF // peers
+    stages = stages_of(peers, lax.axis_size("pix"), lax.axis_size("sub"))
     devices = math.prod(stage[2] for stage in stages)
     blocks = days // BLOCK
     rows = -(-(blocks * (blocks + 1) // 2 * BLOCK) // (8 * devices)) * 8 * devices
@@ -166,17 +226,30 @@
         part //= stage[2]
         landing.append(pltpu.VMEM((stage[2] - 1, part, BLOCK), jnp.float32))
         sems += [pltpu.SemaphoreType.DMA((stage[2] - 1,))] * 4
+    vmem = pl.BlockSpec(memory_space=pltpu.VMEM)
     return pl.pallas_call(
         functools.partial(covariance_kernel, stages),
-        out_shape=jax.ShapeDtypeStruct((days, days), jnp.float32),
-        in_specs=[pl.BlockSpec(memory_space=pltpu.VMEM)],
-        out_specs=pl.BlockSpec(memory_space=pltpu.VMEM),
-        scratch_shapes=[pltpu.VMEM((rows, BLOCK), jnp.float32)] * 2 + landing + sems,
+        out_shape=(
+            jax.ShapeDtypeStruct((days, days), jnp.float32),
+            jax.ShapeDtypeStruct((own, 2 * NB, days), jnp.float32),
+        ),
+        in_specs=[pl.BlockSpec(memory_space=pl.ANY), vmem, vmem],
+        out_specs=(vmem, vmem),
+        scratch_shapes=[
+            pltpu.VMEM((CHUNKS, days, pixels // peers // CHUNKS), jnp.bfloat16),
+            pltpu.VMEM((rows, BLOCK), jnp.float32),
+            pltpu.VMEM((rows, BLOCK), jnp.float32),
+            pltpu.SemaphoreType.DMA((CHUNKS,)),
+            pltpu.SemaphoreType.DMA((CHUNKS, peers - 1)),
+            pltpu.SemaphoreType.DMA((CHUNKS, peers - 1)),
+        ]
+        + landing
+        + sems,
         compiler_params=pltpu.CompilerParams(
-            collective_id=0, has_side_effects=True, vmem_limit_bytes=48 * 2**20
+            collective_id=0, has_side_effects=True, vmem_limit_bytes=56 * 2**20
         ),
         name="covariance",
-    )(series)
+    )(anomaly, offsets[:, None], taper_index[:, None])
 
 
 def leading_kernel(gram_ref, lead_ref):
@@ -204,12 +277,8 @@
 
 
 def shards(anomaly, offsets, taper_index):
-    series = lax.all_to_all(anomaly, "tm", split_axis=1, concat_axis=0, tiled=True)
-    own = NF // lax.axis_size("tm")
-    freqs = lax.axis_index("tm") * own + jnp.arange(own, dtype=jnp.int32)
     total_pixels = anomaly.shape[1] * lax.axis_size(("pix", "sub"))
-    operator = day_operator(offsets, taper_index, freqs, series.shape[0], NFFT)
-    covariance = summed_covariance(series)
+    covariance, operator = covariance_and_operator(anomaly, offsets, taper_index)
     half = jnp.einsum("fid,de->fie", operator, covariance, precision=lax.Precision.HIGH)
     spectral_gram = jnp.einsum("fie,fje->fij", half, operator, precision=lax.Precision.HIGH)
     spectral_gram = spectral_gram / total_pixels

time: 91.4 us -> 90.2 us (0.987)
  Pallas kernels: 26.8 us -> 79.3 us
  waiting for transfers between devices: 41.5 us -> 0 us
  other arithmetic: 7.53 us -> 0 us
  starting transfers between devices: 6.46 us -> 0 us
  matrix products: 3.66 us -> 5.8 us
    pallas_call x1, Pallas kernels: 23.8 us -> 76.4 us  [covariance_and_operator(): pl.pallas_call(functools.partial(covariance_kernel, stages), out_shape=(j...]
    all_to_all x1 -> x0, waiting for transfers between devices: 41.5 us -> none  [shards(): lax.all_to_all(anomaly, 'tm', split_axis=1, concat_axis=0, tiled=True)]
    all_to_all x1 -> x0, starting transfers between devices: 6.46 us -> none  [shards(): lax.all_to_all(anomaly, 'tm', split_axis=1, concat_axis=0, tiled=True)]
    cos x1 -> x0, other arithmetic: 3.82 us -> none  [day_operator(): table = jnp.stack([jnp.cos(angle), -jnp.sin(angle)], axis=1)]
    all_to_all x1 -> x0, local copies, waits for them, and re-layouts: 3.14 us -> none  [shards(): lax.all_to_all(anomaly, 'tm', split_axis=1, concat_axis=0, tiled=True)]
    broadcast_in_dim x0 -> x2, local copies, waits for them, and re-layouts: none -> 2.67 us  [the longest x1 1.34 us: covariance_and_operator(): offsets[:, None]]
    mul x2 -> x0, other arithmetic: 2.42 us -> none  [the longest x1 1.66 us: day_operator(): return (table * scaled).reshape(freqs.shape[0], 2 * offsets.shape[0], days)]
    dot_general x1, matrix products: 1.82 us -> 3.85 us  [shards(): jnp.einsum('fid,de->fie', operator, covariance, precision=lax.Precision.H...]
  transfers between devices with their start and end apart: 1 -> 0, of which waited for: 1 -> 0; matrix products, arithmetic and copies ran while one was open for 8% -> 0% of each run, Pallas kernels for 0% -> 0%
where the time goes in v3:
time: 90.2 us; the launch traced here: 89.8 us
  Pallas kernels  79.3 us (88%)
  matrix products  5.8 us (6%)
  local copies, waits for them, and re-layouts  4 us (4%)
    pallas_call x1, Pallas kernels, covariance_and_operator(): pl.pallas_call(functools.partial(covariance_kernel, stages), out_shape=(j...  76.4 us
    dot_general x1, matrix products, shards(): jnp.einsum('fid,de->fie', operator, covariance, precision=lax.Precision.H...  3.85 us
    pallas_call x1, Pallas kernels, leading_mode(): pl.pallas_call(leading_kernel, out_shape=jax.ShapeDtypeStruct((own, BLOCK...  2.94 us
    dot_general x1, matrix products, shards(): jnp.einsum('fie,fje->fij', half, operator, precision=lax.Precision.HIGH)  1.95 us

profile of v3, /device:TPU:0, one launch (start us, length us, event | category | flops | bytes accessed | tf_op | source)
XLA Modules:
  0.0 89.8 jit_solution(11833083301557096224)
XLA Ops:
  0.6 1.3 %copy.7.offsets = s32[32,1]{1,0:T(8,128)} copy(s32[32,1]{0,1:T(1,128)} %bitcast.8) | data formatting | bytes 256 | tf_op jit(solution)/shard_map/broadcast_in_dim | solution.py:252
  2.0 1.3 %copy.8.taper = s32[32,1]{1,0:T(8,128)} copy(s32[32,1]{0,1:T(1,128)} %bitcast.9) | data formatting | bytes 256 | tf_op jit(solution)/shard_map/broadcast_in_dim | solution.py:252
  3.3 76.4 %covariance.1 = (f32[512,512]{1,0:T(8,128)}, f32[16,64,512]{2,1,0:T(8,128)}) custom-call(bf16[64,16384]{1,0:T(8,128)(2,1)} %anomaly.1, s32[32,1]{1,0:T(8,128)} %copy.7.offsets, s32[32,1]{1,0:T(8,128)} %copy.8.taper), custom_call_target="tpu_custom_call" | custom-call | tf_op jit(solution)/shard_map/covariance/pallas_call | solution.py:230
  79.7 0.0 copy-start
  79.7 3.8 %fusion = f32[16,64,512]{2,1,0:T(8,128)S(1)} fusion(f32[16,64,512]{2,1,0:T(8,128)} %get-tuple-element.4, f32[512,512]{1,0:T(8,128)} %get-tuple-element.5), kind=kOutput, calls=%fused_computation.1 | convolution fusion | flops 1610612736 | bytes 5242880 | tf_op jit(solution)/shard_map/fid,de->fie/dot_general | solution.py:282
  83.6 0.0 copy-done
  83.6 2.0 %convolution_multiply_fusion.gram_ref = f32[16,64,64]{2,1,0:T(8,128)} fusion(f32[16,64,512]{2,1,0:T(8,128)S(1)} %fusion, f32[16,64,512]{2,1,0:T(8,128)S(1)} %copy-done), kind=kOutput, calls=%fused_computation | convolution fusion | flops 201392128 | bytes 4456448 | tf_op jit(solution)/shard_map/fie,fje->fij/dot_general | solution.py:283
  85.5 2.9 %leading.1 = f32[16,128]{1,0:T(8,128)} custom-call(f32[16,64,64]{2,1,0:T(8,128)} %convolution_multiply_fusion.gram_ref), custom_call_target="tpu_custom_call" | custom-call | tf_op jit(solution)/shard_map/leading/pallas_call | solution.py:269
  88.5 1.3 %slice_reduce_fusion = f32[16]{0:T(128)} fusion(f32[16,128]{1,0:T(8,128)} %leading.1), kind=kLoop, calls=%fused_computation.3 | loop fusion | bytes 128 | tf_op jit(solution)/shard_map/slice | solution.py:276
Async XLA Ops:
  79.7 3.9 %copy-start = (f32[16,64,512]{2,1,0:T(8,128)S(1)}, f32[16,64,512]{2,1,0:T(8,128)}, u32[]{:S(2)}) copy-start(f32[16,64,512]{2,1,0:T(8,128)} %get-tuple-element.4) | copy-start | bytes 6291460

commit v4 on v3

--- a/solution.py
+++ b/solution.py
@@ -34,10 +34,17 @@
     return jnp.where((step >= 0) & (step < length), chosen, 0.0)
 
 
+def upright(row):
+    square = (NB, NB)
+    diagonal = lax.broadcasted_iota(jnp.int32, square, 0) == lax.broadcasted_iota(jnp.int32, square, 1)
+    values = jnp.broadcast_to(row[...].astype(jnp.float32), square)
+    return jnp.sum(jnp.where(diagonal, values, 0.0), axis=1, keepdims=True).astype(jnp.int32)
+
+
 def write_operator(offsets, taper, operator):
     own, _, days = operator.shape
-    step = lax.broadcasted_iota(jnp.int32, (NB, days), 1) - offsets[...]
-    windows = windows_of(jnp.broadcast_to(taper[...], (NB, days)), step, NFFT)
+    step = lax.broadcasted_iota(jnp.int32, (NB, days), 1) - upright(offsets)
+    windows = windows_of(jnp.broadcast_to(upright(taper), (NB, days)), step, NFFT)
     scaled = windows * (1.0 / jnp.sqrt(jnp.sum(windows * windows, axis=1, keepdims=True)))
     first = lax.axis_index("tm") * own
 
@@ -59,7 +66,7 @@
         split = [("sub", 1, sub), ("pix", 1, pix), ("tm", 1, tm)]
     else:
         split = [("tm", 1, 2), ("pix", 1, pix), ("tm", 2, tm // 2)]
-    return [stage for stage in split if stage[2] > 1]
+    return split
 
 
 def place_in(stage):
@@ -96,9 +103,7 @@
     stages, anomaly, offsets, taper, out, operator, series, packed, gathered, own_sem, *scratch
 ):
     exchange_send, exchange_recv = scratch[:2]
-    count = len(stages)
-    landing = scratch[2 : 2 + count]
-    sems = scratch[2 + count :]
+    landing, sems = scratch[2:5], scratch[5:]
     chunks, days, width = series.shape
     per_device = anomaly.shape[0]
     peers = days // per_device
@@ -154,53 +159,98 @@
             copy.wait()
         add_products(series.at[chunk], packed, chunk == 0)
 
-    start, rows = 0, packed.shape[0]
-    starts = []
-    for s, stage in enumerate(stages):
-        members = stage[2]
-        part = rows // members
-        starts.append(start)
-        copies = []
-        for shift in range(1, members):
-            device, there = device_at(stage, shift)
-            copy = pltpu.make_async_remote_copy(
-                src_ref=packed.at[pl.ds(pl.multiple_of(start + there * part, 8), part), :],
-                dst_ref=landing[s].at[shift - 1],
-                send_sem=sems[4 * s].at[shift - 1],
-                recv_sem=sems[4 * s + 1].at[shift - 1],
-                device_id=device,
-                device_id_type=MESH,
-            )
-            copy.start()
-            copies.append(copy)
-        start = start + place_in(stage) * part
-        rows = part
-        own = packed.at[pl.ds(pl.multiple_of(start, 8), part), :]
-        total = own[...]
-        for shift in range(1, members):
-            copies[shift - 1].wait()
-            total = total + landing[s][shift - 1]
-        own[...] = total
-    gathered[pl.ds(pl.multiple_of(start, 8), rows), :] = total
-
-    for s in reversed(range(count)):
-        stage = stages[s]
-        own = gathered.at[pl.ds(pl.multiple_of(start, 8), rows), :]
-        copies = []
-        for shift in range(1, stage[2]):
-            copy = pltpu.make_async_remote_copy(
-                src_ref=own,
-                dst_ref=own,
-                send_sem=sems[4 * s + 2].at[shift - 1],
-                recv_sem=sems[4 * s + 3].at[shift - 1],
-                device_id=device_at(stage, shift)[0],
-                device_id_type=MESH,
-            )
-            copy.start()
-            copies.append(copy)
-        for copy in copies:
+    near, side, line = stages
+    piece = packed.shape[0] // line[2]
+    half = piece // near[2]
+    part = half // side[2]
+
+    def rows_of(at, n, s, rows):
+        return pl.ds(pl.multiple_of(at * piece + n * half + s * part, 8), rows)
+
+    def send(src, dst, sem, index, device):
+        copy = pltpu.make_async_remote_copy(
+            src_ref=src,
+            dst_ref=dst,
+            send_sem=sems[2 * sem].at[index],
+            recv_sem=sems[2 * sem + 1].at[index],
+            device_id=device,
+            device_id_type=MESH,
+        )
+        copy.start()
+        return copy
+
+    my_near, my_side = place_in(near), place_in(side)
+    order = list(range(1, line[2])) + [0]
+    order.sort(key=lambda shift: abs(2 * shift - line[2]))
+    targets = {shift: device_at(line, shift) for shift in order}
+
+    near_copies, side_copies, line_copies = {}, {}, {}
+    for shift in order:
+        at = targets[shift][1]
+        near_copies[shift] = []
+        for k in range(1, near[2]):
+            device, there = device_at(near, k)
+            index = shift * (near[2] - 1) + k - 1
+            src = packed.at[rows_of(at, there, 0, half), :]
+            near_copies[shift].append(send(src, landing[0].at[index], 0, index, device))
+    for shift in order:
+        at = targets[shift][1]
+        mine = packed.at[rows_of(at, my_near, 0, half), :]
+        total = mine[...]
+        for k, copy in enumerate(near_copies[shift]):
             copy.wait()
-        start, rows = starts[s], rows * stage[2]
+            total = total + landing[0][shift * (near[2] - 1) + k]
+        mine[...] = total
+        side_copies[shift] = []
+        for k in range(1, side[2]):
+            device, there = device_at(side, k)
+            index = shift * (side[2] - 1) + k - 1
+            src = packed.at[rows_of(at, my_near, there, part), :]
+            side_copies[shift].append(send(src, landing[1].at[index], 1, index, device))
+    for shift in order:
+        device, at = targets[shift]
+        mine = packed.at[rows_of(at, my_near, my_side, part), :]
+        total = mine[...]
+        for k, copy in enumerate(side_copies[shift]):
+            copy.wait()
+            total = total + landing[1][shift * (side[2] - 1) + k]
+        mine[...] = total
+        if shift:
+            line_copies[shift] = send(mine, landing[2].at[shift - 1], 2, shift - 1, device)
+    here = place_in(line)
+    own = gathered.at[rows_of(here, my_near, my_side, part), :]
+    total = packed[rows_of(here, my_near, my_side, part), :]
+    for shift in order:
+        if shift:
+            line_copies[shift].wait()
+            total = total + landing[2][shift - 1]
+    own[...] = total
+
+    arriving = {}
+    for shift in order:
+        if shift:
+            arriving[shift] = send(own, own, 3, shift - 1, targets[shift][0])
+    spread, near_spread = {}, []
+    incoming = [0] + [shift for shift in order if shift]
+    sources = {shift: lax.rem(here + line[2] - shift, line[2]) for shift in incoming}
+    for shift in incoming:
+        if shift:
+            arriving[shift].wait()
+        mine = gathered.at[rows_of(sources[shift], my_near, my_side, part), :]
+        spread[shift] = [
+            send(mine, mine, 4, shift * (side[2] - 1) + k - 1, device_at(side, k)[0])
+            for k in range(1, side[2])
+        ]
+    for shift in incoming:
+        for copy in spread[shift]:
+            copy.wait()
+        mine = gathered.at[rows_of(sources[shift], my_near, 0, half), :]
+        near_spread += [
+            send(mine, mine, 5, shift * (near[2] - 1) + k - 1, device_at(near, k)[0])
+            for k in range(1, near[2])
+        ]
+    for copy in near_spread:
+        copy.wait()
 
     place = 0
     for i in range(blocks):
@@ -221,11 +271,17 @@
     devices = math.prod(stage[2] for stage in stages)
     blocks = days // BLOCK
     rows = -(-(blocks * (blocks + 1) // 2 * BLOCK) // (8 * devices)) * 8 * devices
-    landing, sems, part = [], [], rows
-    for stage in stages:
-        part //= stage[2]
-        landing.append(pltpu.VMEM((stage[2] - 1, part, BLOCK), jnp.float32))
-        sems += [pltpu.SemaphoreType.DMA((stage[2] - 1,))] * 4
+    near, side, line = (stage[2] for stage in stages)
+    half = rows // line // near
+    part = half // side
+    slots = [max(1, count) for count in (line * (near - 1), line * (side - 1), line - 1)]
+    landing = [
+        pltpu.VMEM((count, depth, BLOCK), jnp.float32)
+        for count, depth in zip(slots, (half, part, part))
+    ]
+    sems = [
+        pltpu.SemaphoreType.DMA((slots[stage],)) for stage in (0, 1, 2, 2, 1, 0) for _ in range(2)
+    ]
     vmem = pl.BlockSpec(memory_space=pltpu.VMEM)
     return pl.pallas_call(
         functools.partial(covariance_kernel, stages),
@@ -249,7 +305,7 @@
             collective_id=0, has_side_effects=True, vmem_limit_bytes=56 * 2**20
         ),
         name="covariance",
-    )(anomaly, offsets[:, None], taper_index[:, None])
+    )(anomaly, offsets[None, :], taper_index[None, :])
 
 
 def leading_kernel(gram_ref, lead_ref):

time: 90.2 us -> 84 us (0.931)
  Pallas kernels: 79.3 us -> 76 us
  local copies, waits for them, and re-layouts: 4 us -> 1.33 us
    pallas_call x1, Pallas kernels: 76.4 us -> 73 us  [covariance_and_operator(): pl.pallas_call(functools.partial(covariance_kernel, stages), out_shape=(j...]
    broadcast_in_dim x2 -> x0, local copies, waits for them, and re-layouts: 2.67 us -> none  [the longest x1 1.34 us: covariance_and_operator(): offsets[:, None]]
where the time goes in v4:
time: 84 us; the launch traced here: 83.8 us
  Pallas kernels  76 us (90%)
  matrix products  5.8 us (7%)
  local copies, waits for them, and re-layouts  1.33 us (2%)
    pallas_call x1, Pallas kernels, covariance_and_operator(): pl.pallas_call(functools.partial(covariance_kernel, stages), out_shape=(j...  73 us
    dot_general x1, matrix products, shards(): jnp.einsum('fid,de->fie', operator, covariance, precision=lax.Precision.H...  3.85 us
    pallas_call x1, Pallas kernels, leading_mode(): pl.pallas_call(leading_kernel, out_shape=jax.ShapeDtypeStruct((own, BLOCK...  2.94 us
    dot_general x1, matrix products, shards(): jnp.einsum('fie,fje->fij', half, operator, precision=lax.Precision.HIGH)  1.95 us

profile of v4, /device:TPU:0, one launch (start us, length us, event | category | flops | bytes accessed | tf_op | source)
XLA Modules:
  0.0 83.8 jit_solution(2857313628495302185)
XLA Ops:
  0.6 73.0 %covariance.1 = (f32[512,512]{1,0:T(8,128)}, f32[16,64,512]{2,1,0:T(8,128)}) custom-call(bf16[64,16384]{1,0:T(8,128)(2,1)} %anomaly.1, s32[1,32]{1,0:T(1,128)} %bitcast.8, s32[1,32]{1,0:T(1,128)} %bitcast.9), custom_call_target="tpu_custom_call" | custom-call | tf_op jit(solution)/shard_map/covariance/pallas_call | solution.py:286
  73.7 0.0 copy-start
  73.7 3.8 %fusion = f32[16,64,512]{2,1,0:T(8,128)S(1)} fusion(f32[16,64,512]{2,1,0:T(8,128)} %get-tuple-element.4, f32[512,512]{1,0:T(8,128)} %get-tuple-element.5), kind=kOutput, calls=%fused_computation.1 | convolution fusion | flops 1610612736 | bytes 5242880 | tf_op jit(solution)/shard_map/fid,de->fie/dot_general | solution.py:338
  77.5 0.0 copy-done
  77.5 2.0 %convolution_multiply_fusion.gram_ref = f32[16,64,64]{2,1,0:T(8,128)} fusion(f32[16,64,512]{2,1,0:T(8,128)S(1)} %fusion, f32[16,64,512]{2,1,0:T(8,128)S(1)} %copy-done), kind=kOutput, calls=%fused_computation | convolution fusion | flops 201392128 | bytes 4456448 | tf_op jit(solution)/shard_map/fie,fje->fij/dot_general | solution.py:339
  79.5 2.9 %leading.1 = f32[16,128]{1,0:T(8,128)} custom-call(f32[16,64,64]{2,1,0:T(8,128)} %convolution_multiply_fusion.gram_ref), custom_call_target="tpu_custom_call" | custom-call | tf_op jit(solution)/shard_map/leading/pallas_call | solution.py:325
  82.4 1.3 %slice_reduce_fusion = f32[16]{0:T(128)} fusion(f32[16,128]{1,0:T(8,128)} %leading.1), kind=kLoop, calls=%fused_computation.3 | loop fusion | bytes 128 | tf_op jit(solution)/shard_map/slice | solution.py:332
Async XLA Ops:
  73.7 3.9 %copy-start = (f32[16,64,512]{2,1,0:T(8,128)S(1)}, f32[16,64,512]{2,1,0:T(8,128)}, u32[]{:S(2)}) copy-start(f32[16,64,512]{2,1,0:T(8,128)} %get-tuple-element.4) | copy-start | bytes 6291460

commit v5 on v4

--- a/solution.py
+++ b/solution.py
@@ -41,7 +41,12 @@
     return jnp.sum(jnp.where(diagonal, values, 0.0), axis=1, keepdims=True).astype(jnp.int32)
 
 
-def write_operator(offsets, taper, operator):
+def split(value):
+    high = value.astype(jnp.bfloat16)
+    return high, (value - high.astype(jnp.float32)).astype(jnp.bfloat16)
+
+
+def write_operator(offsets, taper, operator, operator_low):
     own, _, days = operator.shape
     step = lax.broadcasted_iota(jnp.int32, (NB, days), 1) - upright(offsets)
     windows = windows_of(jnp.broadcast_to(upright(taper), (NB, days)), step, NFFT)
@@ -50,8 +55,10 @@
 
     def one(f, carry):
         angle = (((first + f) * step) & (NFFT - 1)).astype(jnp.float32) * (2.0 * math.pi / NFFT)
-        operator[f, :NB, :] = jnp.cos(angle).astype(jnp.bfloat16).astype(jnp.float32) * scaled
-        operator[f, NB:, :] = (-jnp.sin(angle)).astype(jnp.bfloat16).astype(jnp.float32) * scaled
+        for rows, table in ((pl.ds(0, NB), jnp.cos(angle)), (pl.ds(NB, NB), -jnp.sin(angle))):
+            high, low = split(table.astype(jnp.bfloat16).astype(jnp.float32) * scaled)
+            operator[f, rows, :] = high
+            operator_low[f, rows, :] = low
         return carry
 
     lax.fori_loop(0, own, one, 0)
@@ -100,7 +107,7 @@
 
 
 def covariance_kernel(
-    stages, anomaly, offsets, taper, out, operator, series, packed, gathered, own_sem, *scratch
+    stages, anomaly, offsets, taper, out, operator, operator_low, series, packed, gathered, own_sem, *scratch
 ):
     exchange_send, exchange_recv = scratch[:2]
     landing, sems = scratch[2:5], scratch[5:]
@@ -148,7 +155,7 @@
             copies.append(copy)
         exchanged.append(copies)
 
-    write_operator(offsets, taper, operator)
+    write_operator(offsets, taper, operator, operator_low)
     blocks = days // BLOCK
     filled = blocks * (blocks + 1) // 2 * BLOCK
     if packed.shape[0] > filled:
@@ -282,15 +289,18 @@
     sems = [
         pltpu.SemaphoreType.DMA((slots[stage],)) for stage in (0, 1, 2, 2, 1, 0) for _ in range(2)
     ]
+    words = rows * BLOCK * 2 + days * days + own * 2 * NB * days + days * (pixels // peers) // 2
+    words += sum(count * depth * BLOCK for count, depth in zip(slots, (half, part, part)))
     vmem = pl.BlockSpec(memory_space=pltpu.VMEM)
     return pl.pallas_call(
         functools.partial(covariance_kernel, stages),
         out_shape=(
             jax.ShapeDtypeStruct((days, days), jnp.float32),
-            jax.ShapeDtypeStruct((own, 2 * NB, days), jnp.float32),
+            jax.ShapeDtypeStruct((own, 2 * NB, days), jnp.bfloat16),
+            jax.ShapeDtypeStruct((own, 2 * NB, days), jnp.bfloat16),
         ),
-        in_specs=[pl.BlockSpec(memory_space=pl.ANY), vmem, vmem],
-        out_specs=(vmem, vmem),
+        in_specs=[pl.BlockSpec(memory_space=pltpu.HBM), vmem, vmem],
+        out_specs=(vmem, vmem, vmem),
         scratch_shapes=[
             pltpu.VMEM((CHUNKS, days, pixels // peers // CHUNKS), jnp.bfloat16),
             pltpu.VMEM((rows, BLOCK), jnp.float32),
@@ -302,43 +312,74 @@
         + landing
         + sems,
         compiler_params=pltpu.CompilerParams(
-            collective_id=0, has_side_effects=True, vmem_limit_bytes=56 * 2**20
+            collective_id=0, has_side_effects=True, vmem_limit_bytes=4 * words + 8 * 2**20
         ),
         name="covariance",
     )(anomaly, offsets[None, :], taper_index[None, :])
 
 
-def leading_kernel(gram_ref, lead_ref):
-    gram = gram_ref[...]
-    size = gram.shape[1]
-    vector = jnp.ones((gram.shape[0], 1, size), jnp.float32)
+def finish_kernel(pixels, covariance, operator, operator_low, gram, lead, high, low):
+    own, size, days = operator.shape
+    high[...], low[...] = split(covariance[...])
+    group = math.gcd(own, 4)
+
+    def product(left, right, contract):
+        return lax.dot_general(
+            left, right, (((1,), (contract,)), ((), ())), preferred_element_type=jnp.float32
+        )
+
+    for first in range(0, own, group):
+        left = operator[first : first + group].reshape(group * size, days)
+        left_low = operator_low[first : first + group].reshape(group * size, days)
+        half = product(left, high[...], 0) + (
+            product(left_low, high[...], 0) + product(left, low[...], 0)
+        )
+        half_high, half_low = split(half)
+        for f in range(group):
+            rows = slice(f * size, (f + 1) * size)
+            right, right_low = operator[first + f], operator_low[first + f]
+            value = product(half_high[rows], right, 1) + (
+                product(half_low[rows], right, 1) + product(half_high[rows], right_low, 1)
+            )
+            gram[first + f] = value / pixels
+
+    matrix = gram[...]
+    vector = jnp.ones((own, 1, size), jnp.float32)
     for step in range(POWER + 1):
         across = 2 - step % 2
-        applied = jnp.sum(gram * vector, axis=across, keepdims=True)
+        applied = jnp.sum(matrix * vector, axis=across, keepdims=True)
         power = jnp.sum(applied * applied, axis=3 - across, keepdims=True) / size
         vector = applied / jnp.sqrt(power + power_eps)
-    lead_ref[...] = jnp.broadcast_to(jnp.sqrt(power)[:, 0, :], lead_ref.shape)
-
-
-def leading_mode(spectral_gram):
-    own = spectral_gram.shape[0]
-    lead = pl.pallas_call(
-        leading_kernel,
-        out_shape=jax.ShapeDtypeStruct((own, BLOCK), jnp.float32),
-        in_specs=[pl.BlockSpec(memory_space=pltpu.VMEM)],
-        out_specs=pl.BlockSpec(memory_space=pltpu.VMEM),
-        name="leading",
-    )(spectral_gram)
-    return lead[:, 0]
+    column = jnp.broadcast_to(jnp.sqrt(power)[:, 0, :], (own, own))
+    square = (own, own)
+    diagonal = lax.broadcasted_iota(jnp.int32, square, 0) == lax.broadcasted_iota(jnp.int32, square, 1)
+    lead[...] = jnp.sum(jnp.where(diagonal, column, 0.0), axis=0, keepdims=True)
+
+
+def gram_and_leading(covariance, operator, operator_low, pixels):
+    own, size, days = operator.shape
+    vmem = pl.BlockSpec(memory_space=pltpu.VMEM)
+    gram, lead = pl.pallas_call(
+        functools.partial(finish_kernel, pixels),
+        out_shape=(
+            jax.ShapeDtypeStruct((own, size, size), jnp.float32),
+            jax.ShapeDtypeStruct((1, own), jnp.float32),
+        ),
+        in_specs=[vmem] * 3,
+        out_specs=(vmem, vmem),
+        scratch_shapes=[pltpu.VMEM((days, days), jnp.bfloat16)] * 2,
+        compiler_params=pltpu.CompilerParams(
+            vmem_limit_bytes=8 * days * days + 4 * own * size * days + 12 * 2**20
+        ),
+        name="finish",
+    )(covariance, operator, operator_low)
+    return gram, lead[0]
 
 
 def shards(anomaly, offsets, taper_index):
     total_pixels = anomaly.shape[1] * lax.axis_size(("pix", "sub"))
-    covariance, operator = covariance_and_operator(anomaly, offsets, taper_index)
-    half = jnp.einsum("fid,de->fie", operator, covariance, precision=lax.Precision.HIGH)
-    spectral_gram = jnp.einsum("fie,fje->fij", half, operator, precision=lax.Precision.HIGH)
-    spectral_gram = spectral_gram / total_pixels
-    return (spectral_gram, leading_mode(spectral_gram))
+    covariance, operator, operator_low = covariance_and_operator(anomaly, offsets, taper_index)
+    return gram_and_leading(covariance, operator, operator_low, total_pixels)
 
 
 def solution(mesh):

time: 84 us -> 79.4 us (0.945)
  matrix products: 5.8 us -> 0 us
  local copies, waits for them, and re-layouts: 1.33 us -> 2.89 us
    dot_general x2 -> x0, matrix products: 5.8 us -> none  [the longest x1 3.85 us: shards(): jnp.einsum('fid,de->fie', operator, covariance, precision=lax.Precision.H...]
    unnamed x2 -> x6, local copies, waits for them, and re-layouts: 0.01 us -> 2.89 us
    pallas_call x1, Pallas kernels: 73 us -> 70.7 us  [covariance_and_operator(): pl.pallas_call(functools.partial(covariance_kernel, stages), out_shape=(j...]
    pallas_call x1, Pallas kernels: 2.94 us -> 4.98 us  [gram_and_leading(): pl.pallas_call(functools.partial(finish_kernel, pixels), out_shape=(jax.S...]
    slice x1 -> x0, local copies, waits for them, and re-layouts: 1.32 us -> none  [leading_mode(): return lead[:, 0]]
where the time goes in v5:
time: 79.4 us; the launch traced here: 79.2 us
  Pallas kernels  75.6 us (95%)
  local copies, waits for them, and re-layouts  2.89 us (4%)
    pallas_call x1, Pallas kernels, covariance_and_operator(): pl.pallas_call(functools.partial(covariance_kernel, stages), out_shape=(j...  70.7 us
    pallas_call x1, Pallas kernels, gram_and_leading(): pl.pallas_call(functools.partial(finish_kernel, pixels), out_shape=(jax.S...  4.98 us
    unnamed x6, local copies, waits for them, and re-layouts  2.89 us

profile of v5, /device:TPU:0, one launch (start us, length us, event | category | flops | bytes accessed | tf_op | source)
XLA Modules:
  0.0 79.2 jit_solution(15203629644455650457)
XLA Ops:
  0.6 0.0 copy-start
  0.6 1.6 %copy-done = bf16[64,16384]{1,0:T(8,128)(2,1)S(1)} copy-done((bf16[64,16384]{1,0:T(8,128)(2,1)S(1)}, bf16[64,16384]{1,0:T(8,128)(2,1)}, u32[]{:S(2)}) %copy-start) | copy-done | bytes 2097176
  2.2 0.0 copy-start.1
  2.2 0.7 copy-done.1
  2.9 0.0 copy-start.2
  2.9 0.7 copy-done.2
  3.5 70.7 %covariance.1 = (f32[512,512]{1,0:T(8,128)S(1)}, bf16[16,64,512]{2,1,0:T(8,128)(2,1)S(1)}, bf16[16,64,512]{2,1,0:T(8,128)(2,1)S(1)}) custom-call(bf16[64,16384]{1,0:T(8,128)(2,1)S(1)} %copy-done, s32[1,32]{1,0:T(1,128)S(1)} %bitcast.3, s32[1,32]{1,0:T(1,128)S(1)} %bitcast.4), custom_call_target="tpu_custom_call" | custom-call | tf_op jit(solution)/shard_map/covariance/pallas_call | solution.py:295
  74.2 5.0 %finish.1 = (f32[16,64,64]{2,1,0:T(8,128)}, f32[1,16]{1,0:T(1,128)}) custom-call(f32[512,512]{1,0:T(8,128)S(1)} %get-tuple-element.7.covariance, bf16[16,64,512]{2,1,0:T(8,128)(2,1)S(1)} %get-tuple-element.8.operator, bf16[16,64,512]{2,1,0:T(8,128)(2,1)S(1)} %get-tuple-element.9.operator_low), custom_call_target="tpu_custom_call" | custom-call | tf_op jit(solution)/shard_map/finish/pallas_call | solution.py:362
Async XLA Ops:
  0.6 1.6 %copy-start = (bf16[64,16384]{1,0:T(8,128)(2,1)S(1)}, bf16[64,16384]{1,0:T(8,128)(2,1)}, u32[]{:S(2)}) copy-start(bf16[64,16384]{1,0:T(8,128)(2,1)} %anomaly.1) | copy-start | bytes 6291460
  2.2 0.7 copy-start.1
  2.9 0.7 copy-start.2

commit v6 on v4

--- a/solution.py
+++ b/solution.py
@@ -41,7 +41,12 @@
     return jnp.sum(jnp.where(diagonal, values, 0.0), axis=1, keepdims=True).astype(jnp.int32)
 
 
-def write_operator(offsets, taper, operator):
+def split(value):
+    high = value.astype(jnp.bfloat16)
+    return high, (value - high.astype(jnp.float32)).astype(jnp.bfloat16)
+
+
+def write_operator(offsets, taper, operator, operator_low):
     own, _, days = operator.shape
     step = lax.broadcasted_iota(jnp.int32, (NB, days), 1) - upright(offsets)
     windows = windows_of(jnp.broadcast_to(upright(taper), (NB, days)), step, NFFT)
@@ -50,8 +55,10 @@
 
     def one(f, carry):
         angle = (((first + f) * step) & (NFFT - 1)).astype(jnp.float32) * (2.0 * math.pi / NFFT)
-        operator[f, :NB, :] = jnp.cos(angle).astype(jnp.bfloat16).astype(jnp.float32) * scaled
-        operator[f, NB:, :] = (-jnp.sin(angle)).astype(jnp.bfloat16).astype(jnp.float32) * scaled
+        for rows, table in ((pl.ds(0, NB), jnp.cos(angle)), (pl.ds(NB, NB), -jnp.sin(angle))):
+            high, low = split(table.astype(jnp.bfloat16).astype(jnp.float32) * scaled)
+            operator[f, rows, :] = high
+            operator_low[f, rows, :] = low
         return carry
 
     lax.fori_loop(0, own, one, 0)
@@ -80,6 +87,43 @@
     here = place_in(stage)
     there = lax.rem(here + shift, members)
     return {axis: index + (there - here) * inner}, there
+
+
+def finish(pixels, high, low, operator, operator_low, gram, lead):
+    own, size, days = operator.shape
+    group = math.gcd(own, 4)
+
+    def product(left, right, contract):
+        return lax.dot_general(
+            left, right, (((1,), (contract,)), ((), ())), preferred_element_type=jnp.float32
+        )
+
+    for first in range(0, own, group):
+        left = operator[first : first + group].reshape(group * size, days)
+        left_low = operator_low[first : first + group].reshape(group * size, days)
+        half = product(left, high[...], 0) + (
+            product(left_low, high[...], 0) + product(left, low[...], 0)
+        )
+        half_high, half_low = split(half)
+        for f in range(group):
+            rows = slice(f * size, (f + 1) * size)
+            right, right_low = operator[first + f], operator_low[first + f]
+            value = product(half_high[rows], right, 1) + (
+                product(half_low[rows], right, 1) + product(half_high[rows], right_low, 1)
+            )
+            gram[first + f] = value / pixels
+
+    matrix = gram[...]
+    vector = jnp.ones((own, 1, size), jnp.float32)
+    for step in range(POWER + 1):
+        across = 2 - step % 2
+        applied = jnp.sum(matrix * vector, axis=across, keepdims=True)
+        power = jnp.sum(applied * applied, axis=3 - across, keepdims=True) / size
+        vector = applied / jnp.sqrt(power + power_eps)
+    column = jnp.broadcast_to(jnp.sqrt(power)[:, 0, :], (own, own))
+    square = (own, own)
+    diagonal = lax.broadcasted_iota(jnp.int32, square, 0) == lax.broadcasted_iota(jnp.int32, square, 1)
+    lead[...] = jnp.sum(jnp.where(diagonal, column, 0.0), axis=0, keepdims=True)
 
 
 def add_products(series, packed, first):
@@ -100,7 +144,22 @@
 
 
 def covariance_kernel(
-    stages, anomaly, offsets, taper, out, operator, series, packed, gathered, own_sem, *scratch
+    stages,
+    pixels,
+    anomaly,
+    offsets,
+    taper,
+    gram,
+    lead,
+    high,
+    low,
+    operator,
+    operator_low,
+    series,
+    packed,
+    gathered,
+    own_sem,
+    *scratch,
 ):
     exchange_send, exchange_recv = scratch[:2]
     landing, sems = scratch[2:5], scratch[5:]
@@ -148,7 +207,7 @@
             copies.append(copy)
         exchanged.append(copies)
 
-    write_operator(offsets, taper, operator)
+    write_operator(offsets, taper, operator, operator_low)
     blocks = days // BLOCK
     filled = blocks * (blocks + 1) // 2 * BLOCK
     if packed.shape[0] > filled:
@@ -256,17 +315,20 @@
     for i in range(blocks):
         for j in range(i, blocks):
             block = gathered[pl.ds(place * BLOCK, BLOCK), :]
-            out[pl.ds(i * BLOCK, BLOCK), pl.ds(j * BLOCK, BLOCK)] = block
+            upper, lower = pl.ds(i * BLOCK, BLOCK), pl.ds(j * BLOCK, BLOCK)
+            high[upper, lower], low[upper, lower] = split(block)
             if j > i:
-                out[pl.ds(j * BLOCK, BLOCK), pl.ds(i * BLOCK, BLOCK)] = block.T
+                high[lower, upper], low[lower, upper] = split(block.T)
             place += 1
-
-
-def covariance_and_operator(anomaly, offsets, taper_index):
+    finish(pixels, high, low, operator, operator_low, gram, lead)
+
+
+def gram_and_leading(anomaly, offsets, taper_index):
     per_device, pixels = anomaly.shape
     peers = lax.axis_size("tm")
     days = per_device * peers
     own = NF // peers
+    total_pixels = pixels * lax.axis_size(("pix", "sub"))
     stages = stages_of(peers, lax.axis_size("pix"), lax.axis_size("sub"))
     devices = math.prod(stage[2] for stage in stages)
     blocks = days // BLOCK
@@ -284,14 +346,16 @@
     ]
     vmem = pl.BlockSpec(memory_space=pltpu.VMEM)
     return pl.pallas_call(
-        functools.partial(covariance_kernel, stages),
+        functools.partial(covariance_kernel, stages, total_pixels),
         out_shape=(
-            jax.ShapeDtypeStruct((days, days), jnp.float32),
-            jax.ShapeDtypeStruct((own, 2 * NB, days), jnp.float32),
+            jax.ShapeDtypeStruct((own, 2 * NB, 2 * NB), jnp.float32),
+            jax.ShapeDtypeStruct((1, own), jnp.float32),
         ),
         in_specs=[pl.BlockSpec(memory_space=pl.ANY), vmem, vmem],
         out_specs=(vmem, vmem),
-        scratch_shapes=[
+        scratch_shapes=[pltpu.VMEM((days, days), jnp.bfloat16)] * 2
+        + [pltpu.VMEM((own, 2 * NB, days), jnp.bfloat16)] * 2
+        + [
             pltpu.VMEM((CHUNKS, days, pixels // peers // CHUNKS), jnp.bfloat16),
             pltpu.VMEM((rows, BLOCK), jnp.float32),
             pltpu.VMEM((rows, BLOCK), jnp.float32),
@@ -302,43 +366,15 @@
         + landing
         + sems,
         compiler_params=pltpu.CompilerParams(
-            collective_id=0, has_side_effects=True, vmem_limit_bytes=56 * 2**20
+            collective_id=0, has_side_effects=True, vmem_limit_bytes=58 * 2**20
         ),
         name="covariance",
     )(anomaly, offsets[None, :], taper_index[None, :])
 
 
-def leading_kernel(gram_ref, lead_ref):
-    gram = gram_ref[...]
-    size = gram.shape[1]
-    vector = jnp.ones((gram.shape[0], 1, size), jnp.float32)
-    for step in range(POWER + 1):
-        across = 2 - step % 2
-        applied = jnp.sum(gram * vector, axis=across, keepdims=True)
-        power = jnp.sum(applied * applied, axis=3 - across, keepdims=True) / size
-        vector = applied / jnp.sqrt(power + power_eps)
-    lead_ref[...] = jnp.broadcast_to(jnp.sqrt(power)[:, 0, :], lead_ref.shape)
-
-
-def leading_mode(spectral_gram):
-    own = spectral_gram.shape[0]
-    lead = pl.pallas_call(
-        leading_kernel,
-        out_shape=jax.ShapeDtypeStruct((own, BLOCK), jnp.float32),
-        in_specs=[pl.BlockSpec(memory_space=pltpu.VMEM)],
-        out_specs=pl.BlockSpec(memory_space=pltpu.VMEM),
-        name="leading",
-    )(spectral_gram)
-    return lead[:, 0]
-
-
 def shards(anomaly, offsets, taper_index):
-    total_pixels = anomaly.shape[1] * lax.axis_size(("pix", "sub"))
-    covariance, operator = covariance_and_operator(anomaly, offsets, taper_index)
-    half = jnp.einsum("fid,de->fie", operator, covariance, precision=lax.Precision.HIGH)
-    spectral_gram = jnp.einsum("fie,fje->fij", half, operator, precision=lax.Precision.HIGH)
-    spectral_gram = spectral_gram / total_pixels
-    return (spectral_gram, leading_mode(spectral_gram))
+    gram, lead = gram_and_leading(anomaly, offsets, taper_index)
+    return (gram, lead[0])
 
 
 def solution(mesh):

time: 84 us -> 80.2 us (0.955)
  matrix products: 5.8 us -> 0 us
  local copies, waits for them, and re-layouts: 1.33 us -> 2.99 us
    dot_general x2 -> x0, matrix products: 5.8 us -> none  [the longest x1 3.85 us: shards(): jnp.einsum('fid,de->fie', operator, covariance, precision=lax.Precision.H...]
    unnamed x2, local copies, waits for them, and re-layouts: 0.01 us -> 2.99 us
    slice x1 -> x0, local copies, waits for them, and re-layouts: 1.32 us -> none  [leading_mode(): return lead[:, 0]]
    pallas_call x2 -> x1, Pallas kernels: 76 us -> 76.4 us  [gram_and_leading(): pl.pallas_call(functools.partial(covariance_kernel, stages, total_pixels)...]
where the time goes in v6:
time: 80.2 us; the launch traced here: 80.1 us
  Pallas kernels  76.4 us (95%)
  local copies, waits for them, and re-layouts  2.99 us (4%)
    pallas_call x1, Pallas kernels, gram_and_leading(): pl.pallas_call(functools.partial(covariance_kernel, stages, total_pixels)...  76.4 us
    unnamed x2, local copies, waits for them, and re-layouts  2.99 us

profile of v6, /device:TPU:0, one launch (start us, length us, event | category | flops | bytes accessed | tf_op | source)
XLA Modules:
  0.0 80.1 jit_solution(15242598566068035716)
XLA Ops:
  0.6 76.4 %covariance.1 = (f32[16,64,64]{2,1,0:T(8,128)}, f32[1,16]{1,0:T(1,128)}) custom-call(bf16[64,16384]{1,0:T(8,128)(2,1)} %anomaly.1, s32[1,32]{1,0:T(1,128)} %bitcast.3, s32[1,32]{1,0:T(1,128)} %bitcast.4), custom_call_target="tpu_custom_call" | custom-call | tf_op jit(solution)/shard_map/covariance/pallas_call | solution.py:348
  77.1 1.9 %copy.7 = f32[16,64,64]{2,1,0:T(8,128)} copy(f32[16,64,64]{2,1,0:T(8,128)} %get-tuple-element.8) | data formatting | bytes 524288
  79.0 1.1 %copy.8 = f32[16]{0:T(128)} copy(f32[16]{0:T(128)} %bitcast.5) | data formatting | bytes 128
